TPU v7x, 32 devices: a whole 2x2x4 slice. The times are simulated.
32 devices in a mesh: dp: 4 (over z), row: 2 (over x), col: 4 (over y, core).
Axes of the slice: x: 2, y: 2, z: 4, core: 2. Of those that a mesh axis runs over, the one named last changes fastest.
Arguments:
- tokens: bfloat16 [768, 16384], P(('row', 'col'), 'dp'), may hold values from -6 to 6
- cotangent: bfloat16 [768, 16384], P(('row', 'col'), 'dp'), may hold values from -6 to 6
- holder_of: int32 [8, 4], replicated, may hold values from 0 to 3, each once within a row
- lengths: int32 [8, 4, 4], replicated, may hold values from 0 to 512, as said below
- input_gain: float32 [768], P(('row', 'col')), may hold values from 0.5 to 1.5
- input_shift: float32 [768], P(('row', 'col')), may hold values from -1.5 to 1.5
- attend_weight: bfloat16 [3, 768, 768], P(None, 'col', 'row'), may hold values from -0.21875 to 0.21875
- attend_bias: float32 [2, 768], P(None, 'col'), may hold values from -1.5 to 1.5
- mixed_gain: float32 [768], P('col'), may hold values from 0.5 to 1.5
- mixed_shift: float32 [768], P('col'), may hold values from -1.5 to 1.5
- output_weight: bfloat16 [768, 768], P('col', 'row'), may hold values from -0.375 to 0.375
- output_bias: float32 [768], P(('row', 'col')), may hold values from -1.5 to 1.5
- middle_gain: float32 [768], P(('row', 'col')), may hold values from 0.5 to 1.5
- middle_shift: float32 [768], P(('row', 'col')), may hold values from -1.5 to 1.5
- expand_weight: bfloat16 [768, 3072], P('row', 'col'), may hold values from -0.375 to 0.375
- expand_bias: float32 [3072], P('col'), may hold values from -1.5 to 1.5
- hidden_gain: float32 [3072], P('col'), may hold values from 0.5 to 1.5
- hidden_shift: float32 [3072], P('col'), may hold values from -1.5 to 1.5
- shrink_weight: bfloat16 [3072, 768], P('col', 'row'), may hold values from -0.1875 to 0.1875
- shrink_bias: float32 [768], P(('row', 'col')), may hold values from -1.5 to 1.5
Outputs:
- block_out: bfloat16 [768, 16384], P(('row', 'col'), 'dp')
- input_grad: bfloat16 [768, 16384], P(('row', 'col'), 'dp')
- input_gain_grad: float32 [768], P(('row', 'col'))
- input_shift_grad: float32 [768], P(('row', 'col'))
- attend_weight_grad: float32 [3, 768, 768], P(None, 'col', 'row')
- attend_bias_grad: float32 [2, 768], P(None, 'col')
- mixed_gain_grad: float32 [768], P('col')
- mixed_shift_grad: float32 [768], P('col')
- output_weight_grad: float32 [768, 768], P('col', 'row')
- output_bias_grad: float32 [768], P(('row', 'col'))
- middle_gain_grad: float32 [768], P(('row', 'col'))
- middle_shift_grad: float32 [768], P(('row', 'col'))
- expand_weight_grad: float32 [768, 3072], P('row', 'col')
- expand_bias_grad: float32 [3072], P('col')
- hidden_gain_grad: float32 [3072], P('col')
- hidden_shift_grad: float32 [3072], P('col')
- shrink_weight_grad: float32 [3072, 768], P('col', 'row')
- shrink_bias_grad: float32 [768], P(('row', 'col'))
Inputs may be any that keep to these rules, and one draw needn't show every extreme that they name: Each row of holder_of names every holder once. The 4 lengths of a unit add up to 512; a zero length is an empty slot; in every micro-batch one unit is a single sequence of 512 tokens.
All inputs are finite; a program needn't handle non-finite values.
Results may differ from a plain program's by a relative error of at most 0.017.
Values may be sent and summed in bfloat16 or wider, within the bound.
No kernel may reach another device: no remote copies, remote signals or barrier semaphores. Data moves between devices by JAX's collectives and lax.ppermute only.
A program may use at most 128 MiB of HBM per device.

v0:
```python
import functools
import math

import jax
import jax.numpy as jnp
from jax import lax
from jax.experimental import pallas as pl
from jax.experimental.pallas import tpu as pltpu
from jax.sharding import PartitionSpec as P

HEAD = 64
eps = 1e-05
masked_score = -1e30
f32 = jnp.float32
bf16 = jnp.bfloat16
RC = ("row", "col")
HBM = pl.BlockSpec(memory_space=pltpu.HBM)
SMEM = pl.BlockSpec(memory_space=pltpu.SMEM)
VMEM = pl.BlockSpec(memory_space=pltpu.VMEM)
root_half = math.sqrt(0.5)
root_tau = 1.0 / math.sqrt(2.0 * math.pi)
score_scale = 1.0 / math.sqrt(HEAD)


def dot(a, b, ca, cb):
    return lax.dot_general(a, b, (((ca,), (cb,)), ((), ())), preferred_element_type=f32)


def up(v):
    return v.astype(f32)


def lane_sum(v):
    return jnp.sum(v, axis=1, keepdims=True)


def token_sum(v):
    return jnp.sum(v, axis=0, keepdims=True)


CHUNK = 768
ROOM = 8


def over(rows, step, init=0, chunk=CHUNK):
    def one(i, carry):
        return step(pl.ds(pl.multiple_of(i * chunk, chunk), chunk), carry)

    return lax.fori_loop(0, rows // chunk, one, init)


def moments(ref, chunk=CHUNK):
    rows, unit = ref.shape
    zero = jnp.zeros((1, unit), f32)
    mu = over(rows, lambda at, s: s + token_sum(up(ref[at, :])), zero, chunk) * (1.0 / rows)

    def square(at, s):
        d = up(ref[at, :]) - mu
        return s + token_sum(d * d)

    return mu, lax.rsqrt(over(rows, square, zero, chunk) * (1.0 / rows) + eps)


def norm(out, ref, pd, gain, shift):
    mu, r = moments(ref, CHUNK // 2)

    def one(at, carry):
        out[at, :] = ((up(ref[at, :]) - mu) * r * pd[at, gain : gain + 1] + pd[at, shift : shift + 1]).astype(bf16)
        return carry

    over(ref.shape[0], one, chunk=CHUNK // 2)


def norm_back(grad, ref, pd, gain, gd, emit):
    rows, unit = ref.shape
    mu, r = moments(ref, CHUNK // 2)
    zero = jnp.zeros((1, unit), f32)

    def first(at, s):
        g = grad[at, :]
        gv = g * ((up(ref[at, :]) - mu) * r)
        gd[at, 0:1] = lane_sum(gv)
        gd[at, 1:2] = lane_sum(g)
        k = pd[at, gain : gain + 1]
        return s[0] + token_sum(g * k), s[1] + token_sum(gv * k)

    m1, m2 = over(rows, first, (zero, zero))
    m1, m2 = m1 * (1.0 / rows), m2 * (1.0 / rows)

    def second(at, carry):
        vh = (up(ref[at, :]) - mu) * r
        emit(at, r * (grad[at, :] * pd[at, gain : gain + 1] - m1 - vh * m2))
        return carry

    over(rows, second)


PIECES = ((0, None), (1, None), (2, None), (3, None), (4, None), (5, None), (6, 0), (6, 1), (7, 0), (7, 1))


def fetch(pieces, rows, parts):
    for ref, (block, half) in zip(pieces, PIECES):
        first, last = (0, rows) if half is None else (half * rows // 2, (half + 1) * rows // 2)
        for lo, hi, place, sem in parts:
            a, b = max(lo, first), min(hi, last)
            if a < b:
                pltpu.make_async_copy(
                    ref.at[pl.ds(a - first, b - a)], place(block).at[pl.ds(a - lo, b - a)], sem.at[block]
                ).start()


def arrive(ref, sem):
    pltpu.make_async_copy(ref, ref, sem).wait()


def move(src, dst, sem):
    copy = pltpu.make_async_copy(src, dst, sem)
    copy.start()
    return copy


def vmem_bytes(shape, dtype):
    size = jnp.dtype(dtype).itemsize
    sublanes, lanes = 32 // size, 128
    *lead, rows, columns = (1,) * max(0, 2 - len(shape)) + tuple(shape)
    return math.prod(lead) * (-(-rows // sublanes) * sublanes) * (-(-columns // lanes) * lanes) * size


def pinned(spec):
    return pltpu.VMEM if spec is VMEM else pltpu.HBM


def call(kernel, outs, in_specs, out_specs, scratch=(), flops=0, moved=0, name=None, aliases=None):
    held = [v for v in scratch if v.memory_space == pltpu.VMEM]
    limit = sum(vmem_bytes(v.shape, v.dtype) for v in held) + (ROOM << 20)
    single = not isinstance(outs, tuple)
    places = [pinned(spec)(v.shape, v.dtype) for v, spec in zip((outs,) if single else outs, (out_specs,) if single else out_specs)]

    def run(*args):
        args = [v if spec is SMEM else pltpu.with_memory_space_constraint(v, pinned(spec)) for v, spec in zip(args, in_specs)]
        return pl.pallas_call(
            kernel,
            out_shape=places[0] if single else tuple(places),
            in_specs=in_specs,
            out_specs=out_specs,
            scratch_shapes=list(scratch),
            compiler_params=pltpu.CompilerParams(vmem_limit_bytes=limit),
            cost_estimate=pl.CostEstimate(flops=flops, bytes_accessed=moved, transcendentals=0),
            name=name,
            input_output_aliases=aliases or {},
        )(*args)

    return run


def sds(shape, dtype):
    return jax.ShapeDtypeStruct(shape, dtype)


def segment_rows(info, unit):
    t = lax.broadcasted_iota(jnp.int32, (16, unit), 1)
    slot = lax.broadcasted_iota(jnp.int32, (16, unit), 0)
    one = lambda b: jnp.where(t >= b, 1, 0)
    seg = one(info[2]) + one(info[3]) + one(info[4])
    same = seg == slot
    for_keys = jnp.where(same, 1.0, 0.0)
    for_queries = jnp.where(jnp.logical_and(slot < 4, jnp.logical_not(same)), masked_score, 0.0)
    return for_keys, for_queries


def split3(v):
    hi = v.astype(bf16)
    v = v - up(hi)
    mid = v.astype(bf16)
    return hi, mid, (v - up(mid)).astype(bf16)


def three_rows(base, v, first):
    row = lax.broadcasted_iota(jnp.int32, base.shape, 0)
    for i, part in enumerate(split3(v)):
        base = jnp.where(row == first + i, up(part), base)
    return base


def unit_of(ref, which):
    blocks, n, rows, _ = ref.shape
    rows //= 2
    return jnp.concatenate(
        [
            jnp.concatenate([ref[k, i, which * rows : (which + 1) * rows, :] for i in range(n)], axis=0)
            for k in range(blocks)
        ],
        axis=1,
    )


def apart(ref, at, value):
    width = ref.shape[2]
    for i in range(ref.shape[0]):
        ref[i, at, :] = value[:, i * width : (i + 1) * width]


def beside(ref, info, nc, rw):
    def place(i):
        row = jnp.bitwise_xor(info[1], i // nc)
        return ref.at[i % nc, :, pl.ds(pl.multiple_of(row * rw, rw), rw)]

    return place


def below(ref, info, nc, rw):
    def place(i):
        row = jnp.bitwise_xor(info[1], i // nc)
        return ref.at[i % nc, pl.ds(pl.multiple_of(row * rw, rw), rw)]

    return place


def attend_kernel(nc, hw, rw, fl, fw, info, both, even, odd, *refs):
    pieces = refs[:10]
    x_ref, a_ref, qkv_out, lse_ref, o_ref, pd, pf = refs[10:17]
    qkv_ref, ga, ka, qa, ga_sem, out_sem = refs[17:]
    unit = o_ref.shape[1]
    fetch(pieces, 4 * hw, ((0, 3 * hw, beside(ga, info, nc, rw), ga_sem),))
    for i in range(2 * nc):
        tile = (even, odd)[i % 2][i // 2]
        pd[pl.ds(pl.multiple_of(jnp.bitwise_xor(info[0], i) * fl, fl), fl), 0:6] = tile[:, 0:6]
        if i < nc:
            for k in range(hw // fl):
                pd[i * hw + k * fl : i * hw + (k + 1) * fl, 6:10] = tile[:, 6 + 4 * k : 10 + 4 * k]
            for k in range(fw // fl):
                first = 6 + 4 * (hw // fl) + 3 * k
                pf[i, k * fl : (k + 1) * fl, 0:3] = tile[:, first : first + 3]
    x_ref[...] = unit_of(both, 0)
    norm(a_ref, x_ref, pd, 0, 1)
    for_keys, for_queries = segment_rows(info, unit)
    ka[HEAD:, :] = for_keys.astype(bf16)
    qa[HEAD:, :] = for_queries.astype(bf16)

    def per_block(c, carry):
        for i in (c, nc + c):
            arrive(ga.at[c, :, pl.ds(0, rw)], ga_sem.at[i])
        trip = dot(ga[c], a_ref[...], 1, 0)
        at = pl.multiple_of(c * hw, hw)
        qkv_ref[c, 0:hw, :] = (trip[0:hw] + pd[pl.ds(at, hw), 6:7]).astype(bf16)
        qkv_ref[c, hw : 2 * hw, :] = trip[hw : 2 * hw].astype(bf16)
        qkv_ref[c, 2 * hw :, :] = (trip[2 * hw :] + pd[pl.ds(at, hw), 7:8]).astype(bf16)
        move(qkv_ref.at[c], qkv_out.at[c], out_sem.at[c])
        for h in range(hw // HEAD):
            qa[0:HEAD, :] = qkv_ref[c, h * HEAD : (h + 1) * HEAD, :] * jnp.bfloat16(score_scale)
            ka[0:HEAD, :] = qkv_ref[c, hw + h * HEAD : hw + (h + 1) * HEAD, :]
            v = qkv_ref[c, 2 * hw + h * HEAD : 2 * hw + (h + 1) * HEAD, :]
            s = dot(ka[...], qa[...], 0, 0)
            top = jnp.max(s, axis=0, keepdims=True)
            e = jnp.exp(s - top)
            den = token_sum(e)
            o = dot(v, e.astype(bf16), 1, 0) * (1.0 / den)
            o_ref[pl.ds(pl.multiple_of(c * hw + h * HEAD, HEAD), HEAD), :] = o
            lse_ref[c, h : h + 1, :] = top + jnp.log(den)
        return carry

    lax.fori_loop(0, nc, per_block, 0)
    for c in range(nc):
        arrive(qkv_ref.at[c], out_sem.at[c])


def output_kernel(nc, hw, rw, info, x_ref, o_ref, pd, *refs):
    pieces = refs[:10]
    on_ref, x1_ref, b_ref, go, go_sem = refs[10:]
    fetch(pieces, 4 * hw, ((3 * hw, 4 * hw, lambda i: go.at[i // nc, pl.ds(i % nc * hw, hw)], go_sem),))
    my_row = info[1]
    norm(on_ref, o_ref, pd, 8, 9)
    for i in range(2 * nc):
        arrive(go.at[i // nc, pl.ds(i % nc * hw, hw)], go_sem.at[i])

    def one(r, carry):
        rows = pl.ds(pl.multiple_of(r * rw, rw), rw)
        x1_ref[rows, :] = dot(go[jnp.bitwise_xor(my_row, r)], on_ref[...], 0, 0) + up(x_ref[rows, :]) + pd[rows, 2:3]
        return carry

    lax.fori_loop(0, 2, one, 0)
    norm(b_ref, x1_ref, pd, 3, 4)


def expand_kernel(nc, rw, fw, info, b_ref, pf, *refs):
    pieces = refs[:10]
    gn_ref, vh_out, slope_out, st_ref = refs[10:14]
    vh_ref, slope_ref, g_ref, ge, ge_sem, out_sem = refs[14:]
    fetch(pieces, rw, ((0, rw, below(ge, info, nc, rw), ge_sem),))
    unit = b_ref.shape[1]
    total = nc * fw

    def first(c, s):
        for i in (c, nc + c):
            arrive(ge.at[c, pl.ds(0, rw)], ge_sem.at[i])
        f = dot(ge[c], b_ref[...], 0, 0) + pf[c, :, 0:1]
        phi = 0.5 * (1.0 + lax.erf(f * root_half))
        g = f * phi
        g_ref[c] = g
        slope_ref[c] = (phi + f * (jnp.exp(-0.5 * f * f) * root_tau)).astype(bf16)
        move(slope_ref.at[c], slope_out.at[c], out_sem.at[c])
        return s + token_sum(g)

    mu = lax.fori_loop(0, nc, first, jnp.zeros((1, unit), f32)) * (1.0 / total)

    def second(c, s):
        def square(at, t):
            d = g_ref[c, at, :] - mu
            return t + token_sum(d * d)

        return over(fw, square, s)

    r = lax.rsqrt(lax.fori_loop(0, nc, second, jnp.zeros((1, unit), f32)) * (1.0 / total) + eps)
    st_ref[...] = jnp.broadcast_to(r, st_ref.shape)

    def third(c, carry):
        def one(at, t):
            vh = (g_ref[c, at, :] - mu) * r
            vh_ref[c, at, :] = vh.astype(bf16)
            gn_ref[c, at, :] = (vh * pf[c, at, 1:2] + pf[c, at, 2:3]).astype(bf16)
            return t

        over(fw, one)
        move(vh_ref.at[c], vh_out.at[c], out_sem.at[nc + c])
        return carry

    lax.fori_loop(0, nc, third, 0)
    for c in range(nc):
        arrive(slope_ref.at[c], out_sem.at[c])
        arrive(vh_ref.at[c], out_sem.at[nc + c])


def store_blocks(nc, blocks, keep, send):
    def one(k, carry):
        for ref, c in ((send, 2 * k + 1), (keep, 2 * k)):
            blocks(c, lambda row: ref.at[row, k])
        return carry

    lax.fori_loop(0, nc // 2, one, 0)


def shrink_grads_kernel(nc, rw, info, gn_ref, both, e2_ref, keep, send):
    my_row = info[1]
    e2_ref[...] = unit_of(both, 1)

    def blocks(c, place):
        grad = dot(gn_ref[c], e2_ref[...], 1, 1).astype(bf16)
        for r in range(2):
            place(jnp.bitwise_xor(my_row, r))[...] = grad[:, r * rw : (r + 1) * rw]

    store_blocks(nc, blocks, keep, send)


def add_blocks(left, right, outs):
    h = left.shape[2] // 2
    for j in range(4):
        r, c = j // 2, j % 2
        outs[r][c] = (up(left[r, c, :h]) + up(right[r, c, :h])).astype(bf16)
        outs[2 + c][r] = (up(left[r, c, h:]) + up(right[r, c, h:])).astype(bf16)


def hidden_back_kernel(nc, rw, fw, info, st_ref, e2_ref, pf, left, right, vh_in, slope_in, *refs):
    pieces = refs[:10]
    df_ref, gf_ref, p0, p1, q0, q1 = refs[10:16]
    vh_ref, slope_ref, gs, dgn, gs_sem, vh_sem, slope_sem = refs[16:]
    fetch(pieces, fw, ((0, fw, beside(gs, info, nc, rw), gs_sem),))
    for c in range(nc):
        move(vh_in.at[c], vh_ref.at[c], vh_sem.at[c])
    for c in range(nc):
        move(slope_in.at[c], slope_ref.at[c], slope_sem.at[c])
    add_blocks(left, right, (p0, p1, q0, q1))
    r = st_ref[0:1, :]
    unit = e2_ref.shape[1]
    total = nc * fw

    def first(c, s):
        for i in (c, nc + c):
            arrive(gs.at[c, :, pl.ds(0, rw)], gs_sem.at[i])
        arrive(vh_ref.at[c], vh_sem.at[c])
        dgn[c] = dot(gs[c], e2_ref[...], 1, 0)

        def one(at, t):
            d = dgn[c, at, :]
            dv = d * up(vh_ref[c, at, :])
            gf_ref[c, at, 0:1] = lane_sum(dv)
            gf_ref[c, at, 1:2] = lane_sum(d)
            gain = pf[c, at, 1:2]
            return t[0] + token_sum(d * gain), t[1] + token_sum(dv * gain)

        return over(fw, one, s)

    zero = jnp.zeros((1, unit), f32)
    m1, m2 = lax.fori_loop(0, nc, first, (zero, zero))
    m1, m2 = m1 * (1.0 / total), m2 * (1.0 / total)

    def second(c, carry):
        arrive(slope_ref.at[c], slope_sem.at[c])

        def one(at, t):
            dg = r * (dgn[c, at, :] * pf[c, at, 1:2] - m1 - up(vh_ref[c, at, :]) * m2)
            df = (dg * up(slope_ref[c, at, :])).astype(bf16)
            df_ref[c, at, :] = df
            gf_ref[c, at, 2:3] = lane_sum(up(df))
            return t

        over(fw, one)
        return carry

    lax.fori_loop(0, nc, second, 0)


def middle_back_kernel(nc, rw, fw, info, df_ref, x1_ref, e2_ref, pd, *refs):
    pieces = refs[:10]
    dx1_ref, e1_ref, gd_ref, ge, db, ge_sem = refs[10:]
    fetch(pieces, rw, ((0, rw, below(ge, info, nc, rw), ge_sem),))
    db[...] = jnp.zeros(db.shape, f32)

    def one(c, carry):
        for i in (c, nc + c):
            arrive(ge.at[c, pl.ds(0, rw)], ge_sem.at[i])
        db[...] += dot(ge[c], df_ref[c], 1, 0)
        return carry

    lax.fori_loop(0, nc, one, 0)

    def emit(at, dx):
        dy = up(e2_ref[at, :])
        dx1 = dy + dx
        dx1_ref[at, :] = dx1
        e1 = dx1.astype(bf16)
        e1_ref[at, :] = e1
        gd_ref[at, 2:3] = lane_sum(up(e1))
        gd_ref[at, 3:4] = lane_sum(dy)

    norm_back(db, x1_ref, pd, 3, gd_ref, emit)


def middle_grads_kernel(
    nc, hw, rw, fw, info, b_ref, df_ref, on_ref, e1_ref, keep, send,
):
    my_row = info[1]

    def blocks(c, place):
        grad = dot(b_ref[...], df_ref[c], 1, 1).astype(bf16)
        out_grad = dot(on_ref[c], e1_ref[...], 1, 1).astype(bf16)
        half = fw // 2
        for r in range(2):
            ref = place(jnp.bitwise_xor(my_row, r))
            for k in range(2):
                ref[k * rw : (k + 1) * rw, :] = grad[r * rw : (r + 1) * rw, k * half : (k + 1) * half]
            ref[2 * rw :, :] = out_grad[:, r * rw : (r + 1) * rw]

    store_blocks(nc, blocks, keep, send)


def heads_back(first, last, hw, info, qkv_ref, lse_ref, o_ref, do_ref, dqkv_ref, gh_ref, ka, qa, va, oa):
    unit = o_ref.shape[1]
    for_keys, for_queries = segment_rows(info, unit)
    slot = lax.broadcasted_iota(jnp.int32, (16, unit), 0)
    ka[HEAD:, :] = jnp.where(jnp.logical_and(slot >= 4, slot < 7), 1.0, for_keys).astype(bf16)
    va[HEAD:, :] = jnp.where(slot < 3, 1.0, 0.0).astype(bf16)
    nothing = jnp.zeros((16, unit), f32)

    def per_block(c, carry):
        to = lambda j, h: pl.ds(pl.multiple_of(c * 3 * hw + j * hw + h * HEAD, HEAD), HEAD)
        for h in range(hw // HEAD):
            rows = pl.ds(pl.multiple_of(c * hw + h * HEAD, HEAD), HEAD)
            q = qkv_ref[c, h * HEAD : (h + 1) * HEAD, :] * jnp.bfloat16(score_scale)
            k = qkv_ref[c, hw + h * HEAD : hw + (h + 1) * HEAD, :]
            d = do_ref[rows, :]
            inner = jnp.sum(up(d) * o_ref[rows, :], axis=0, keepdims=True)
            qa[0:HEAD, :] = q
            qa[HEAD:, :] = three_rows(for_queries, -lse_ref[c, h : h + 1, :], 4).astype(bf16)
            ka[0:HEAD, :] = k
            va[0:HEAD, :] = qkv_ref[c, 2 * hw + h * HEAD : 2 * hw + (h + 1) * HEAD, :]
            oa[0:HEAD, :] = d
            oa[HEAD:, :] = three_rows(nothing, -inner, 0).astype(bf16)
            p = jnp.exp(dot(ka[...], qa[...], 0, 0))
            ds = (p * dot(va[...], oa[...], 0, 0)).astype(bf16)
            dv = dot(d, p.astype(bf16), 1, 1).astype(bf16)
            dq = (dot(k, ds, 1, 0) * score_scale).astype(bf16)
            dk = dot(q, ds, 1, 1).astype(bf16)
            dqkv_ref[to(0, h), :] = dq
            dqkv_ref[to(1, h), :] = dk
            dqkv_ref[to(2, h), :] = dv
            gh_ref[c, h * HEAD : (h + 1) * HEAD, 0:1] = lane_sum(up(dq))
            gh_ref[c, h * HEAD : (h + 1) * HEAD, 1:2] = lane_sum(up(dv))
        return carry

    lax.fori_loop(first, last, per_block, 0)


def attend_back_kernel(nc, hw, rw, info, e1_ref, o_ref, lse_ref, pd, left, right, qkv_in, *refs):
    pieces = refs[:10]
    dqkv_ref, gd_ref, gh_ref, do_ref, qkv_ref, p0, p1, q0, q1, go, don, ka, qa, va, oa, go_sem, in_sem = refs[10:]
    qkv_copy = move(qkv_in, qkv_ref, in_sem)

    def place(i):
        row = jnp.bitwise_xor(info[1], i // nc)
        return go.at[pl.ds(i % nc * hw, hw), pl.ds(pl.multiple_of(row * rw, rw), rw)]

    fetch(pieces, 4 * hw, ((3 * hw, 4 * hw, place, go_sem),))
    add_blocks(left, right, (p0, p1, q0, q1))
    for i in range(2 * nc):
        arrive(go.at[pl.ds(0, hw), pl.ds(0, rw)], go_sem.at[i])
    don[...] = dot(go[...], e1_ref[...], 1, 0)

    def emit(at, dx):
        do_ref[at, :] = dx.astype(bf16)

    norm_back(don, o_ref, pd, 8, gd_ref, emit)
    qkv_copy.wait()
    heads_back(0, nc // 2, hw, info, qkv_ref, lse_ref, o_ref, do_ref, dqkv_ref, gh_ref, ka, qa, va, oa)


def attend_back_rest_kernel(nc, hw, info, o_ref, qkv_ref, lse_ref, do_ref, _, __, dqkv_ref, gh_ref, ka, qa, va, oa):
    heads_back(nc // 2, nc, hw, info, qkv_ref, lse_ref, o_ref, do_ref, dqkv_ref, gh_ref, ka, qa, va, oa)


def input_back_kernel(nc, hw, rw, info, dqkv, x_ref, dx1_ref, pd, *refs):
    pieces = refs[:10]
    outs_ref, gd_ref, ga, da, ga_sem = refs[10:]

    def place(i):
        row = jnp.bitwise_xor(info[1], i // nc)
        c = i % nc
        rows = pl.ds(c % 2 * 3 * hw, 3 * hw)
        return ga.at[c // 2, rows, pl.ds(pl.multiple_of(row * rw, rw), rw)]

    fetch(pieces, 4 * hw, ((0, 3 * hw, place, ga_sem),))
    for i in range(2 * nc):
        arrive(ga.at[0, pl.ds(0, 3 * hw), pl.ds(0, rw)], ga_sem.at[i])
    da[...] = jnp.zeros(da.shape, f32)

    def one(k, carry):
        rows = pl.ds(pl.multiple_of(k * 6 * hw, 6 * hw), 6 * hw)
        da[...] += dot(ga[k], dqkv[rows, :], 0, 0)
        return carry

    lax.fori_loop(0, nc // 2, one, 0)

    def emit(at, dx):
        apart(outs_ref, at, (dx1_ref[at, :] + dx).astype(bf16))

    norm_back(da, x_ref, pd, 0, gd_ref, emit)


def attend_grads_kernel(
    nc, hw, rw, fl, fw, info, dqkv, a_ref, gd_in, gd_mid, gd_mix, gh, gf_ref, keep, send, wide, thin,
):
    my_row = info[1]
    lane = lax.broadcasted_iota(jnp.int32, (fl, 128), 1)

    def own(i, carry):
        at = pl.ds(pl.multiple_of(i * fl, fl), fl)
        tile = jnp.zeros((fl, 128), f32)
        for k, (ref, j) in enumerate(((gd_in, 0), (gd_in, 1), (gd_mid, 2), (gd_mid, 0), (gd_mid, 1), (gd_mid, 3))):
            tile = jnp.where(lane == k, ref[at, j : j + 1], tile)
        wide[at, :] = tile
        return carry

    lax.fori_loop(0, 2 * nc, own, 0)

    def columns(c, carry):
        tile = jnp.zeros((fl, 128), f32)
        at = 6
        for k in range(hw // fl):
            rows = slice(k * fl, (k + 1) * fl)
            deep = pl.ds(pl.multiple_of(c * hw + k * fl, fl), fl)
            for column in (gh[c, rows, 0:1], gh[c, rows, 1:2], gd_mix[deep, 0:1], gd_mix[deep, 1:2]):
                tile = jnp.where(lane == at, column, tile)
                at += 1
        for k in range(fw // fl):
            rows = slice(k * fl, (k + 1) * fl)
            for column in (gf_ref[c, rows, 2:3], gf_ref[c, rows, 0:1], gf_ref[c, rows, 1:2]):
                tile = jnp.where(lane == at, column, tile)
                at += 1
        thin[c] = tile
        return carry

    lax.fori_loop(0, nc, columns, 0)

    def blocks(c, place):
        grad = dot(dqkv[pl.ds(pl.multiple_of(c * 3 * hw, 3 * hw), 3 * hw), :], a_ref[...], 1, 1).astype(bf16)
        for row in range(2):
            place(jnp.bitwise_xor(my_row, row))[0 : 3 * hw, :] = grad[:, row * rw : (row + 1) * rw]
        for row in range(2):
            block = jnp.bitwise_xor(info[0], row * nc + c)
            tile = thin[c] + wide[pl.ds(pl.multiple_of(block * fl, fl), fl), :]
            third = fl // 3
            tile = jnp.concatenate([tile[m * third : (m + 1) * third] for m in range(3)], axis=1)
            place(row)[3 * hw :, :] = tile.astype(bf16)

    store_blocks(nc, blocks, keep, send)


def shrink_kernel(nc, rw, fw, info, pd, gn_ref, x1_ref, *refs):
    pieces = refs[:10]
    y_ref, gs, gs_sem = refs[10:]
    fetch(pieces, fw, ((0, fw, lambda i: gs.at[i // nc, pl.ds(i % nc * fw, fw)], gs_sem),))
    my_row = info[1]
    for i in range(2 * nc):
        arrive(gs.at[i // nc, pl.ds(i % nc * fw, fw)], gs_sem.at[i])

    def one(r, carry):
        rows = pl.ds(pl.multiple_of(r * rw, rw), rw)
        part = dot(gs[jnp.bitwise_xor(my_row, r)], gn_ref[...], 0, 0)
        apart(y_ref, rows, (x1_ref[rows, :] + part + pd[rows, 5:6]).astype(bf16))
        return carry

    lax.fori_loop(0, 2, one, 0)


def body(
    tokens,
    cotangent,
    holder_of,
    lengths,
    input_gain,
    input_shift,
    attend_weight,
    attend_bias,
    mixed_gain,
    mixed_shift,
    output_weight,
    output_bias,
    middle_gain,
    middle_shift,
    expand_weight,
    expand_bias,
    hidden_gain,
    hidden_shift,
    shrink_weight,
    shrink_bias,
):
    holders = lax.axis_size("dp")
    half = holders // 2
    nr, nc = lax.axis_size("row"), lax.axis_size("col")
    n = nr * nc
    micro = holder_of.shape[0]
    assert micro == n and nr == 2 and nc == 4
    fl = tokens.shape[0]
    pairs = micro * half
    blk = tokens.shape[1] // pairs
    unit = half * blk
    dp = lax.axis_index("dp")
    side, pos = dp // half, dp % half
    my_row, my_col = lax.axis_index("row"), lax.axis_index("col")
    rc = my_row * nc + my_col
    groups = [list(range(s * half * n, (s + 1) * half * n)) for s in range(2)]
    hw, rw, fw = output_weight.shape[0], output_weight.shape[1], shrink_weight.shape[0]

    def flip_row(v):
        return lax.ppermute(v, "row", [(i, i ^ 1) for i in range(nr)])

    def flip_chip(v):
        return lax.ppermute(v, "col", [(i, i ^ 2) for i in range(nc)])

    def flip_core(v):
        return lax.ppermute(v, "col", [(i, i ^ 1) for i in range(nc)])

    def flip_dp(v, step):
        return lax.ppermute(v, "dp", [(i, i ^ step) for i in range(holders)])

    def exchange(v):
        return lax.all_to_all(v, ("dp",) + RC, 0, 0, axis_index_groups=groups, tiled=True)

    lanes = blk % 128 == 0

    def by_target(v):
        v = jnp.transpose(v.reshape(2, fl, half * n, blk), (2, 0, 1, 3))
        return v.reshape(half * n, 2 * fl, blk)

    def exchange_units(v):
        v = exchange(v).reshape(half, n, 2 * fl, blk)
        return v if lanes else jnp.transpose(v, (1, 2, 0, 3)).reshape(1, n, 2 * fl, unit)

    def from_unit(v):
        if not lanes:
            v = jnp.transpose(v.reshape(n * fl, half, blk), (1, 0, 2))
        v = exchange(v.reshape(half * n, fl, blk))
        return jnp.transpose(v, (1, 0, 2)).reshape(tokens.shape)

    def tie(*values):
        return lax.optimization_barrier(values)

    def near(v):
        return flip_row(v), flip_chip(v)

    def far(v, by_row, by_chip):
        h = v.shape[0] // 2
        return flip_row(by_chip[:h]), flip_chip(by_row[h:])

    def near_flips(v, near_v):
        return tuple(flip_core(p) for p in (v, near_v[1], near_v[0]))

    def pieces_of(v, near_v, flips, far_v):
        v1, c1, r1 = flips
        f1, g1 = (flip_core(p) for p in far_v)
        return (v, v1, near_v[1], c1, near_v[0], r1, far_v[0], far_v[1], f1, g1)

    w1 = jnp.concatenate([attend_weight.reshape(3 * hw, rw), output_weight], axis=0)
    near1 = near(w1)
    tile = jnp.concatenate(
        [
            jnp.stack([input_gain, input_shift, output_bias, middle_gain, middle_shift, shrink_bias]),
            jnp.transpose(
                jnp.stack([attend_bias[0], attend_bias[1], mixed_gain, mixed_shift]).reshape(4, -1, fl), (1, 0, 2)
            ).reshape(-1, fl),
            jnp.transpose(jnp.stack([expand_bias, hidden_gain, hidden_shift]).reshape(3, -1, fl), (1, 0, 2)).reshape(-1, fl),
        ]
    )
    tile = jnp.transpose(jnp.pad(tile, ((0, 128 - tile.shape[0]), (0, 0))))
    ready = by_target(jnp.concatenate([tokens, cotangent], axis=0))
    near1, tile, ready = tie(near1, tile, ready)
    far1 = far(w1, *near1)
    both = exchange_units(ready)
    tile_row, tile_chip = near(tile)
    even = jnp.stack([tile, tile_chip, tile_row, flip_row(tile_chip)])
    odd = flip_core(even)
    flips1 = near_flips(w1, near1)
    far1, flips1, both, odd, w2 = tie(far1, flips1, both, odd, expand_weight)
    near2 = near(w2)
    g1 = pieces_of(w1, near1, flips1, far1)

    k_unit = 2 * (pos * n + rc) + side
    own = lengths[k_unit // holders, holder_of[k_unit // holders, k_unit % holders]]
    info = jnp.concatenate([jnp.stack([rc, my_row]), jnp.cumsum(own)[:-1]]).astype(jnp.int32)

    d = n * fl
    split = lambda v: v.reshape(nr, rw, unit)
    dma = pltpu.SemaphoreType.DMA
    weight_flops = 2 * unit * d * nc * fw

    dp_odd = dp % 2 == 1

    def reduce_rest(v):
        step = 2
        while 2 * step < holders:
            v = v + flip_dp(v, step)
            step *= 2
        return v, flip_dp(v, step) if step < holders else jnp.zeros_like(v)

    def spread(v):
        return v, flip_dp(v, 1)

    def whole(v, got):
        return jnp.concatenate([jnp.where(dp_odd, got, v), jnp.where(dp_odd, v, got)], axis=0).astype(f32)

    vm = lambda shape, dtype=bf16: pltpu.VMEM(shape, dtype)
    act, act32, hid = (d, unit), (nc * hw, unit), (nc, fw, unit)
    part1, part2, part3 = (nr, nc // 2, 4 * hw, rw), (nr, nc // 2, rw, fw), (nr, nc // 2, fw, rw)

    def time_us(t):
        return dict(flops=int(t * 1e9), moved=int(t * 1e6))

    extra = vm((HEAD + 16, unit))
    x, a, qkv, lse, o, pd, pf = call(
        functools.partial(attend_kernel, nc, hw, rw, fl, fw),
        (
            sds(act, bf16), sds(act, bf16), sds((nc, 3 * hw, unit), bf16), sds((nc, 8, unit), f32), sds(act, f32),
            sds((d, 16), f32), sds((nc, fw, 8), f32),
        ),
        [SMEM] + [VMEM] * 3 + [HBM] * 10,
        [VMEM, VMEM, HBM, VMEM, VMEM, VMEM, VMEM],
        [
            vm((nc, 3 * hw, unit)), vm((nc, 3 * hw, nr * rw)), extra, extra,
            dma((n,)), dma((nc,)),
        ],
        **time_us(13), name="attend",
    )(info, both, even, odd, *g1)

    o, near2 = tie(o, near2)
    far2 = far(w2, *near2)
    flips2 = near_flips(w2, near2)

    on, x1, b = call(
        functools.partial(output_kernel, nc, hw, rw),
        (sds(act, bf16), sds(act, f32), sds(act, bf16)),
        [SMEM] + [VMEM] * 3 + [HBM] * 10,
        [VMEM] * 3,
        [vm((nr, nc * hw, rw)), dma((n,))],
        **time_us(5), name="output",
    )(info, x, o, pd, *g1)

    b, far2, flips2, w3 = tie(b, far2, flips2, shrink_weight)
    near3 = near(w3)
    g2 = pieces_of(w2, near2, flips2, far2)

    gn, vh, slope, st = call(
        functools.partial(expand_kernel, nc, rw, fw),
        (sds(hid, bf16), sds(hid, bf16), sds(hid, bf16), sds((8, unit), f32)),
        [SMEM, VMEM, VMEM] + [HBM] * 10,
        [VMEM, HBM, HBM, VMEM],
        [vm(hid), vm(hid), vm(hid, f32), vm((nc, nr * rw, fw)), dma((n,)), dma((2 * nc,))],
        **time_us(13), name="expand",
    )(info, b, pf, *g2)

    gn, near3 = tie(gn, near3)
    far3 = far(w3, *near3)
    flips3 = near_flips(w3, near3)

    e2, shr_keep, shr_send = call(
        functools.partial(shrink_grads_kernel, nc, rw),
        (sds(act, bf16), sds(part3, bf16), sds(part3, bf16)),
        [SMEM] + [VMEM] * 2,
        [VMEM] * 3,
        **time_us(7), name="shrink_grads",
    )(info, gn, both)

    shr_send, far3, flips3 = tie(shr_send, far3, flips3)
    g3 = pieces_of(w3, near3, flips3, far3)
    shr_got = flip_core(shr_send)

    def reduce_near(v):
        return flip_row(v[1]), flip_chip(v[3])

    def reduce_far(v, got):
        p, q = v[0] + got[0], v[2] + got[1]
        return (p[0], q[0]), (flip_chip(p[1]), flip_row(q[1]))

    def reduce_dp(v, got):
        p, q = v[0] + got[0], v[1] + got[1]
        return jnp.where(dp_odd, q, p), flip_dp(jnp.where(dp_odd, p, q), 1)

    sum3 = (nc // 2, fw // 2, rw)
    df, gf, *shr = call(
        functools.partial(hidden_back_kernel, nc, rw, fw),
        (sds(hid, bf16), sds((nc, fw, 8), f32)) + (sds(sum3, bf16),) * 4,
        [SMEM] + [VMEM] * 5 + [HBM] * 12,
        [VMEM] * 6,
        [vm(hid), vm(hid), vm((nc, fw, nr * rw)), vm(hid, f32), dma((n,)), dma((nc,)), dma((nc,))],
        **time_us(13), name="hidden_back",
    )(info, st, e2, pf, shr_keep, shr_got, vh, slope, *g3)

    shr_near = reduce_near(shr)

    dx1, e1, gd_mid = call(
        functools.partial(middle_back_kernel, nc, rw, fw),
        (sds(act, f32), sds(act, bf16), sds((d, 8), f32)),
        [SMEM] + [VMEM] * 4 + [HBM] * 10,
        [VMEM] * 3,
        [vm((nc, nr * rw, fw)), vm(act, f32), dma((n,))],
        **time_us(8), name="middle_back",
    )(info, df, x1, e2, pd, *g2)

    rows2 = 2 * rw + hw
    part2 = (nr, nc // 2, rows2, rw)
    sum2 = (nc // 2, rows2 // 2, rw)
    mid_keep, mid_send = call(
        functools.partial(middle_grads_kernel, nc, hw, rw, fw),
        (sds(part2, bf16), sds(part2, bf16)),
        [SMEM] + [VMEM] * 4,
        [VMEM] * 2,
        **time_us(7), name="middle_grads",
    )(info, b, df, on.reshape(nc, hw, unit), e1)

    e1, mid_send, shr_near = tie(e1, mid_send, shr_near)
    mid_got = flip_core(mid_send)
    shr_stay, shr_far = reduce_far(shr, shr_near)

    all_heads = (nc * 3 * hw, unit)
    dqkv, gd_mix, gh, do, qkv, *mid = call(
        functools.partial(attend_back_kernel, nc, hw, rw),
        (sds(all_heads, bf16), sds((d, 8), f32), sds((nc, hw, 8), f32), sds(act, bf16), sds(qkv.shape, bf16))
        + (sds(sum2, bf16),) * 4,
        [SMEM] + [VMEM] * 6 + [HBM] * 11,
        [VMEM] * 9,
        [vm((nc * hw, nr * rw)), vm(act, f32), extra, extra, extra, extra, dma((n,)), dma(())],
        **time_us(11), name="attend_back",
    )(info, e1, o, lse, pd, mid_keep, mid_got, qkv, *g1)

    do, shr_far, mid = tie(do, shr_far, mid)
    shr, shr_dp = reduce_dp(shr_stay, shr_far)
    mid_near = reduce_near(mid)

    dqkv, gh = call(
        functools.partial(attend_back_rest_kernel, nc, hw),
        (sds(all_heads, bf16), sds((nc, hw, 8), f32)),
        [SMEM] + [VMEM] * 6,
        [VMEM] * 2,
        [extra, extra, extra, extra],
        **time_us(8), name="attend_back_rest", aliases={5: 0, 6: 1},
    )(info, o, qkv, lse, do, dqkv, gh)

    dqkv, shr_dp = tie(dqkv, shr_dp)
    shr, shr_rest = reduce_rest(shr + shr_dp)

    input_grad, gd_in = call(
        functools.partial(input_back_kernel, nc, hw, rw),
        (sds((half if lanes else 1, d, blk if lanes else unit), bf16), sds((d, 8), f32)),
        [SMEM] + [VMEM] * 4 + [HBM] * 10,
        [VMEM] * 2,
        [vm((2, nc // 2 * 3 * hw, nr * rw)), vm(act, f32), dma((n,))],
        **time_us(7), name="input_back",
    )(info, dqkv, x, dx1, pd, *g1)

    gd_in, mid_near = tie(gd_in, mid_near)
    mid_stay, mid_far = reduce_far(mid, mid_near)

    rows1 = 3 * hw + fl // 3
    part1 = (nr, nc // 2, rows1, rw)
    att_keep, att_send = call(
        functools.partial(attend_grads_kernel, nc, hw, rw, fl, fw),
        (sds(part1, bf16), sds(part1, bf16)),
        [SMEM] + [VMEM] * 7,
        [VMEM] * 2,
        [vm((d, 128), f32), vm((nc, fl, 128), f32)],
        **time_us(7), name="attend_grads",
    )(info, dqkv, a, gd_in, gd_mid, gd_mix, gh, gf)

    att_send, shr_rest, mid_far = tie(att_send, shr_rest, mid_far)
    att_got = flip_core(att_send)
    mid, mid_dp = reduce_dp(mid_stay, mid_far)
    shr, shr_got = spread(shr + shr_rest)
    h = rows1 // 2
    p1, q1 = att_keep[1, :, :h] + att_got[1, :, :h], att_keep[:, 1, h:] + att_got[:, 1, h:]
    p1, q1, y_in = tie(p1, q1, gn)
    p_row, q_chip = flip_row(p1), flip_chip(q1)

    y = call(
        functools.partial(shrink_kernel, nc, rw, fw),
        sds(input_grad.shape, bf16),
        [SMEM] + [VMEM] * 3 + [HBM] * 10,
        VMEM,
        [vm((nr, nc * fw, rw)), dma((n,))],
        **time_us(8), name="shrink",
    )(info, pd, y_in.reshape(nc * fw, unit), x1, *g3)

    y, mid_dp, shr_got, input_grad = tie(y, mid_dp, shr_got, input_grad)
    mid, mid_rest = reduce_rest(mid + mid_dp)
    mid, p_row, q_chip = tie(mid, p_row, q_chip)
    p = att_keep[0, :, :h] + att_got[0, :, :h] + p_row
    q = att_keep[:, 0, h:] + att_got[:, 0, h:] + q_chip
    att_far = flip_chip(p[1]), flip_row(q[1])
    input_grad = from_unit(input_grad)
    att, att_dp = reduce_dp((p[0], q[0]), att_far)
    att_dp, mid_rest, y = tie(att_dp, mid_rest, y)
    block_out = from_unit(y)
    att, att_rest = reduce_rest(att + att_dp)
    mid, mid_got = spread(mid + mid_rest)
    att, att_got = spread(att + att_rest)
    att_got, mid_got, shr_got = tie(att_got, mid_got, shr_got)
    att, mid, shr_w_g = whole(att, att_got), whole(mid, mid_got), whole(shr, shr_got)
    exp_w_g = jnp.concatenate([mid[:rw], mid[rw : 2 * rw]], axis=1)

    thin = att[3 * hw :]
    thin = jnp.transpose(jnp.concatenate([thin[:, k * 128 : (k + 1) * 128] for k in range(3)], axis=0))
    in_g_g, in_s_g, out_b_g, mid_g_g, mid_s_g, shr_b_g = (thin[i] for i in range(6))
    at = 6 + 4 * (hw // fl)
    heads_g = jnp.transpose(thin[6:at].reshape(-1, 4, fl), (1, 0, 2)).reshape(4, hw)
    hidden_g = jnp.transpose(thin[at : at + 3 * (fw // fl)].reshape(-1, 3, fl), (1, 0, 2)).reshape(3, fw)
    q_b_g, v_b_g, mix_g_g, mix_s_g = heads_g
    exp_b_g, hid_g_g, hid_s_g = hidden_g
    return (
        block_out,
        input_grad,
        in_g_g,
        in_s_g,
        att[: 3 * hw].reshape(attend_weight.shape),
        jnp.stack([q_b_g, v_b_g]),
        mix_g_g,
        mix_s_g,
        mid[2 * rw :],
        out_b_g,
        mid_g_g,
        mid_s_g,
        exp_w_g,
        exp_b_g,
        hid_g_g,
        hid_s_g,
        shr_w_g,
        shr_b_g,
    )


def solution(mesh):
    wide, narrow = P(RC), P("col")
    in_specs = (
        P(RC, "dp"), P(RC, "dp"), P(), P(), wide, wide, P(None, "col", "row"), P(None, "col"),
        narrow, narrow, P("col", "row"), wide, wide, wide, P("row", "col"), narrow, narrow, narrow,
        P("col", "row"), wide,
    )
    out_specs = (
        P(RC, "dp"), P(RC, "dp"), wide, wide, P(None, "col", "row"), P(None, "col"), narrow, narrow,
        P("col", "row"), wide, wide, wide, P("row", "col"), narrow, narrow, narrow, P("col", "row"),
        wide,
    )
    return jax.shard_map(body, mesh=mesh, in_specs=in_specs, out_specs=out_specs, check_vma=False)
```

profile of v0, /device:TPU:0, one launch (start us, length us, event | category | flops | bytes accessed | tf_op | source)
XLA Modules:
  0.0 283.0 jit_solution(7084131441669857810)
XLA Ops:
  1.9 3.0 %collective-permute-start.1 = (bf16[768,384]{1,0:T(8,128)(2,1)S(1)}, bf16[768,384]{1,0:T(8,128)(2,1)}, u32[]{:S(2)}, u32[]{:S(2)}) collective-permute-start(bf16[768,384]{1,0:T(8,128)(2,1)S(1)} %pad_maximum_fusion.2.refs_0_), channel_id=1, source_target_pairs={{0,2},{1,3},{2,0},{3,1},{4,6},{5,7},{6,4},{7,5},{8,10},{9,11},{10,... | collective-permute-start | bytes 1769480 | tf_op jit(solution)/shard_map/ppermute | solution.py:657
  15.2 3.2 %collective-permute-done.1.refs_2_ = bf16[768,384]{1,0:T(8,128)(2,1)} collective-permute-done((bf16[768,384]{1,0:T(8,128)(2,1)S(1)}, bf16[768,384]{1,0:T(8,128)(2,1)}, u32[]{:S(2)}, u32[]{:S(2)}) %collective-permute-start.1) | collective-permute-done | bytes 589856 | tf_op jit(solution)/shard_map/ppermute | solution.py:657
  19.8 3.9 %all-to-all-start = ((bf16[16,192,256]{2,1,0:T(8,128)(2,1)}), bf16[16,192,256]{2,1,0:T(8,128)(2,1)S(1)}, u32[]{:S(2)}, u32[]{:S(2)}) async-start(bf16[16,192,256]{2,1,0:T(8,128)(2,1)} %bitcast.18), calls=%async_computation | async-start | bytes 3145728 | tf_op jit(solution)/shard_map/all_to_all | solution.py:666
  27.9 14.8 %collective-permute-done.7 = f32[96,128]{1,0:T(8,128)S(1)} collective-permute-done((f32[96,128]{1,0:T(8,128)S(1)}, f32[96,128]{1,0:T(8,128)S(1)}, u32[]{:S(2)}, u32[]{:S(2)}) %collective-permute-start.7) | collective-permute-done | bytes 49184 | tf_op jit(solution)/shard_map/ppermute | solution.py:657
  42.7 3.6 %collective-permute-start.9 = (f32[96,128]{1,0:T(8,128)S(1)}, f32[96,128]{1,0:T(8,128)S(1)}, u32[]{:S(2)}, u32[]{:S(2)}) collective-permute-start(f32[96,128]{1,0:T(8,128)S(1)} %collective-permute-done.7), channel_id=1, source_target_pairs={{0,4},{4,0},{1,5},{5,1},{2,6},{6,2},{3,7},{7,3},{8,12},{12,8},{9,1... | collective-permute-start | bytes 147464 | tf_op jit(solution)/shard_map/ppermute | solution.py:654
  59.9 11.8 %attend.1 = (bf16[768,512]{1,0:T(8,128)(2,1)S(1)}, bf16[768,512]{1,0:T(8,128)(2,1)S(1)}, bf16[4,576,512]{2,1,0:T(8,128)(2,1)}, f32[4,8,512]{2,1,0:T(8,128)S(1)},...) custom-call(s32[5]{0:T(128)S(1)} %pad_add_fusion.info, ...), custom_call_target="tpu_custom_call" | custom-call | flops 12999999488 | bytes 13000000 | tf_op jit(solution)/shard_map/attend/pallas_call | solution.py:141
  76.7 3.8 %output.1 = (bf16[768,512]{1,0:T(8,128)(2,1)S(1)}, f32[768,512]{1,0:T(8,128)S(1)}, bf16[768,512]{1,0:T(8,128)(2,1)S(1)}) custom-call(s32[5]{0:T(128)S(1)} %pad_add_fusion.info, bf16[768,512]{1,0:T(8,128)(2,1)S(1)} %get-tuple-element.142.x_ref, f32[768,512]{1,0:T(8,128)S(1)} %get-tuple-element.141.o_ref, f32[768,16]{1,0:T(8,128)S(1)} %get-tuple-element.143.pd, ...), custom_call_target="tpu_custom_call" | custom-call | flops 5000000000 | bytes 5000000 | tf_op jit(solution)/shard_map/output/pallas_call | solution.py:141
  80.5 2.6 collective-permute-done.16.refs_7_
  87.3 11.5 %expand.1 = (bf16[4,768,512]{2,1,0:T(8,128)(2,1)S(1)}, bf16[4,768,512]{2,1,0:T(8,128)(2,1)}, bf16[4,768,512]{2,1,0:T(8,128)(2,1)}, f32[8,512]{1,0:T(8,128)S(1)}) custom-call(s32[5]{0:T(128)S(1)} %pad_add_fusion.info, bf16[768,512]{1,0:T(8,128)(2,1)S(1)} %get-tuple-element.147.b_ref, f32[4,768,8]{2,1,0:T(8,128)S(1)} %get-tuple-element.148.pf, ...), custom_call_target="tpu_custom_call" | custom-call | flops 12999999488 | bytes 13000000 | tf_op jit(solution)/shard_map/expand/pallas_call | solution.py:141
  104.1 3.5 %shrink_grads.1 = (bf16[768,512]{1,0:T(8,128)(2,1)S(1)}, bf16[2,2,768,384]{3,2,1,0:T(8,128)(2,1)S(1)}, bf16[2,2,768,384]{3,2,1,0:T(8,128)(2,1)S(1)}) custom-call(s32[5]{0:T(128)S(1)} %pad_add_fusion.info, bf16[4,768,512]{2,1,0:T(8,128)(2,1)S(1)} %get-tuple-element.220.gn_ref, bf16[2,8,192,256]{3,2,1,0:T(8,128)(2,1)S(1)} %bitcast.131), custom_call_target="tpu_custom_call" | custom-call | flops 7000000000 | bytes 7000000 | tf_op jit(solution)/shard_map/shrink_grads/pallas_call | solution.py:141
  107.7 2.9 %collective-permute-done.25.refs_7_ = bf16[384,384]{1,0:T(8,128)(2,1)S(1)} collective-permute-done((bf16[384,384]{1,0:T(8,128)(2,1)S(1)}, bf16[384,384]{1,0:T(8,128)(2,1)S(1)}, u32[]{:S(2)}, u32[]{:S(2)}) %collective-permute-start.25) | collective-permute-done | bytes 294944 | tf_op jit(solution)/shard_map/ppermute | solution.py:657
  111.8 4.4 %collective-permute-done.30.refs_8_ = bf16[384,384]{1,0:T(8,128)(2,1)S(1)} collective-permute-done((bf16[384,384]{1,0:T(8,128)(2,1)S(1)}, bf16[384,384]{1,0:T(8,128)(2,1)S(1)}, u32[]{:S(2)}, u32[]{:S(2)}) %collective-permute-start.30) | collective-permute-done | bytes 294944 | tf_op jit(solution)/shard_map/ppermute | solution.py:660
  117.3 10.3 %hidden_back.1 = (bf16[4,768,512]{2,1,0:T(8,128)(2,1)S(1)}, f32[4,768,8]{2,1,0:T(8,128)S(1)}, bf16[2,384,384]{2,1,0:T(8,128)(2,1)S(1)}, bf16[2,384,384]{2,1,0:T(...) custom-call(s32[5]{0:T(128)S(1)} %pad_add_fusion.info, ...), custom_call_target="tpu_custom_call" | custom-call | flops 12999999488 | bytes 13000000 | tf_op jit(solution)/shard_map/hidden_back/pallas_call | solution.py:141
  129.8 7.5 %middle_back.1 = (f32[768,512]{1,0:T(8,128)S(1)}, bf16[768,512]{1,0:T(8,128)(2,1)S(1)}, f32[768,8]{1,0:T(8,128)S(1)}) custom-call(s32[5]{0:T(128)S(1)} %pad_add_fusion.info, bf16[4,768,512]{2,1,0:T(8,128)(2,1)S(1)} %get-tuple-element.171.df_ref, f32[768,512]{1,0:T(8,128)S(1)} %get-tuple-element.172.x1_ref, bf16[768,512]{1,0:T(8,128)(2,1)S(1)} %get-tuple-element.158.e2_ref, ...), custom_call_target="tpu_custom_call" | custom-call | flops 8000000000 | bytes 8000000 | tf_op jit(solution)/shard_map/middle_back/pallas_call | solution.py:141
  139.3 5.9 %middle_grads.1 = (bf16[2,2,960,384]{3,2,1,0:T(8,128)(2,1)S(1)}, bf16[2,2,960,384]{3,2,1,0:T(8,128)(2,1)}) custom-call(s32[5]{0:T(128)S(1)} %pad_add_fusion.info, bf16[768,512]{1,0:T(8,128)(2,1)S(1)} %get-tuple-element.147.b_ref, bf16[4,768,512]{2,1,0:T(8,128)(2,1)S(1)} %get-tuple-element.171.df_ref, bf16[4,192,512]{2,1,0:T(8,128)(2,1)S(1)} %bitcast.133, ...), custom_call_target="tpu_custom_call" | custom-call | flops 7000000000 | bytes 7000000 | tf_op jit(solution)/shard_map/middle_grads/pallas_call | solution.py:141
  156.4 10.2 %attend_back.1 = (bf16[2304,512]{1,0:T(8,128)(2,1)S(1)}, f32[768,8]{1,0:T(8,128)S(1)}, f32[4,192,8]{2,1,0:T(8,128)S(1)}, bf16[768,512]{1,0:T(8,128)(2,1)S(1)}, b...) custom-call(s32[5]{0:T(128)S(1)} %pad_add_fusion.info, ...), custom_call_target="tpu_custom_call" | custom-call | flops 11000000512 | bytes 11000000 | tf_op jit(solution)/shard_map/attend_back/pallas_call | solution.py:141
  170.3 4.8 %attend_back_rest.1 = (bf16[2304,512]{1,0:T(8,128)(2,1)S(1)}, f32[4,192,8]{2,1,0:T(8,128)S(1)}) custom-call(s32[5]{0:T(128)S(1)} %pad_add_fusion.info, f32[768,512]{1,0:T(8,128)S(1)} %copy-done.5, bf16[4,576,512]{2,1,0:T(8,128)(2,1)S(1)} %get-tuple-element.183.qkv_ref, ...), custom_call_target="tpu_custom_call", output_to_operand_aliasing={{0}: (5, {}), {1}: (6, {})} | custom-call | flops 8000000000 | bytes 8000000 | tf_op jit(solution)/shard_map/attend_back_rest/pallas_call | solution.py:141
  176.5 2.6 collective-permute-start.40
  179.1 8.3 %input_back.1 = (bf16[2,768,256]{2,1,0:T(8,128)(2,1)}, f32[768,8]{1,0:T(8,128)S(1)}) custom-call(s32[5]{0:T(128)S(1)} %pad_add_fusion.info, bf16[2304,512]{1,0:T(8,128)(2,1)S(1)} %get-tuple-element.199.dqkv, bf16[768,512]{1,0:T(8,128)(2,1)S(1)} %copy-done.9, f32[768,512]{1,0:T(8,128)S(1)} %copy-done.11, f32[768,16]{1,0:T(8,128)S(1)} %copy-done.16, ...), custom_call_target="tpu_custom_call" | custom-call | flops 7000000000 | bytes 7000000 | tf_op jit(solution)/shard_map/input_back/pallas_call | solution.py:141
  190.4 6.2 %attend_grads.1 = (bf16[2,2,608,384]{3,2,1,0:T(8,128)(2,1)S(1)}, bf16[2,2,608,384]{3,2,1,0:T(8,128)(2,1)S(1)}) custom-call(s32[5]{0:T(128)S(1)} %pad_add_fusion.info, bf16[2304,512]{1,0:T(8,128)(2,1)S(1)} %get-tuple-element.199.dqkv, bf16[768,512]{1,0:T(8,128)(2,1)S(1)} %copy-done.20, f32[768,8]{1,0:T(8,128)S(1)} %get-tuple-element.205.gd_in, ...), custom_call_target="tpu_custom_call" | custom-call | flops 7000000000 | bytes 7000000 | tf_op jit(solution)/shard_map/attend_grads/pallas_call | solution.py:141
  204.4 6.6 %shrink.1 = bf16[2,768,256]{2,1,0:T(8,128)(2,1)} custom-call(s32[5]{0:T(128)S(1)} %pad_add_fusion.info, f32[768,16]{1,0:T(8,128)S(1)} %copy-done.16, bf16[3072,512]{1,0:T(8,128)(2,1)S(1)} %bitcast.132, f32[768,512]{1,0:T(8,128)S(1)} %get-tuple-element.172.x1_ref, bf16[768,384]{1,0:T(8,128)(2,1)} %refs_0_.3, bf16[768,384]{1,0:T(8,128)(2,1)} %copy-done.40, ...), custom_call_target="tpu_custom_call" | custom-call | flops 8000000000 | bytes 8000000 | tf_op jit(solution)/shard_map/shrink/pallas_call | solution.py:141
  211.0 5.0 %collective-permute-done.44 = bf16[480,384]{1,0:T(8,128)(2,1)S(1)} collective-permute-done((bf16[480,384]{1,0:T(8,128)(2,1)S(1)}, bf16[480,384]{1,0:T(8,128)(2,1)S(1)}, u32[]{:S(2)}, u32[]{:S(2)}) %collective-permute-start.44) | collective-permute-done | bytes 368672 | tf_op jit(solution)/shard_map/ppermute | solution.py:663
  220.7 3.1 %collective-permute-done.48 = bf16[304,384]{1,0:T(8,128)(2,1)S(1)} collective-permute-done((bf16[304,384]{1,0:T(8,128)(2,1)S(1)}, bf16[304,384]{1,0:T(8,128)(2,1)S(1)}, u32[]{:S(2)}, u32[]{:S(2)}) %collective-permute-start.48) | collective-permute-done | bytes 233504 | tf_op jit(solution)/shard_map/ppermute | solution.py:657
  225.8 3.9 %all-to-all-start.2 = ((bf16[16,96,256]{2,1,0:T(8,128)(2,1)}), bf16[16,96,256]{2,1,0:T(8,128)(2,1)S(1)}, u32[]{:S(2)}, u32[]{:S(2)}) async-start(bf16[16,96,256]{2,1,0:T(8,128)(2,1)} %bitcast.44), calls=%async_computation.2 | async-start | bytes 1572864 | tf_op jit(solution)/shard_map/all_to_all | solution.py:666
  229.6 7.2 %collective-permute-done.51 = bf16[480,384]{1,0:T(8,128)(2,1)S(1)} collective-permute-done((bf16[480,384]{1,0:T(8,128)(2,1)S(1)}, bf16[480,384]{1,0:T(8,128)(2,1)S(1)}, u32[]{:S(2)}, u32[]{:S(2)}) %collective-permute-start.51) | collective-permute-done | bytes 368672 | tf_op jit(solution)/shard_map/ppermute | solution.py:663
  236.8 2.9 %collective-permute-done.50 = bf16[304,384]{1,0:T(8,128)(2,1)} collective-permute-done((bf16[304,384]{1,0:T(8,128)(2,1)}, bf16[304,384]{1,0:T(8,128)(2,1)}, u32[]{:S(2)}, u32[]{:S(2)}) %collective-permute-start.50) | collective-permute-done | bytes 233504 | tf_op jit(solution)/shard_map/ppermute | solution.py:663
  242.0 2.5 collective-permute-start.54
  244.5 6.3 %collective-permute-done.52 = bf16[304,384]{1,0:T(8,128)(2,1)S(1)} collective-permute-done((bf16[304,384]{1,0:T(8,128)(2,1)S(1)}, bf16[304,384]{1,0:T(8,128)(2,1)S(1)}, u32[]{:S(2)}, u32[]{:S(2)}) %collective-permute-start.52) | collective-permute-done | bytes 233504 | tf_op jit(solution)/shard_map/ppermute | solution.py:663
  251.1 9.8 %collective-permute-done.54 = bf16[480,384]{1,0:T(8,128)(2,1)S(1)} collective-permute-done((bf16[480,384]{1,0:T(8,128)(2,1)S(1)}, bf16[480,384]{1,0:T(8,128)(2,1)S(1)}, u32[]{:S(2)}, u32[]{:S(2)}) %collective-permute-start.54) | collective-permute-done | bytes 368672 | tf_op jit(solution)/shard_map/ppermute | solution.py:663
  260.9 3.6 %collective-permute-done.53 = bf16[304,384]{1,0:T(8,128)(2,1)S(1)} collective-permute-done((bf16[304,384]{1,0:T(8,128)(2,1)S(1)}, bf16[304,384]{1,0:T(8,128)(2,1)S(1)}, u32[]{:S(2)}, u32[]{:S(2)}) %collective-permute-start.53) | collective-permute-done | bytes 233504 | tf_op jit(solution)/shard_map/ppermute | solution.py:663
  265.0 3.7 %all-to-all-start.1 = ((bf16[16,96,256]{2,1,0:T(8,128)(2,1)}), bf16[16,96,256]{2,1,0:T(8,128)(2,1)S(1)}, u32[]{:S(2)}, u32[]{:S(2)}) async-start(bf16[16,96,256]{2,1,0:T(8,128)(2,1)} %bitcast.42), calls=%async_computation.1 | async-start | bytes 1572864 | tf_op jit(solution)/shard_map/all_to_all | solution.py:666
  278.7 3.4 %all-to-all-done.1 = bf16[16,96,256]{2,1,0:T(8,128)(2,1)S(1)} async-done(((bf16[16,96,256]{2,1,0:T(8,128)(2,1)}), bf16[16,96,256]{2,1,0:T(8,128)(2,1)S(1)}, u32[]{:S(2)}, u32[]{:S(2)}) %all-to-all-start.1) | async-done | bytes 786464 | tf_op jit(solution)/shard_map/all_to_all | solution.py:666
  (291 shorter events, 96.7 us)
Async XLA Ops:
  1.9 16.5 %collective-permute-start.1 = (bf16[768,384]{1,0:T(8,128)(2,1)S(1)}, bf16[768,384]{1,0:T(8,128)(2,1)}, u32[]{:S(2)}, u32[]{:S(2)}) collective-permute-start(bf16[768,384]{1,0:T(8,128)(2,1)S(1)} %pad_maximum_fusion.2.refs_0_), channel_id=1, source_target_pairs={{0,2},{1,3},{2,0},{3,1},{4,6},{5,7},{6,4},{7,5},{8,10},{9,11},{10,... | collective-permute-start | bytes 1769480 | tf_op jit(solution)/shard_map/ppermute | solution.py:657
  5.0 14.9 %collective-permute-start = (bf16[768,384]{1,0:T(8,128)(2,1)S(1)}, bf16[768,384]{1,0:T(8,128)(2,1)}, u32[]{:S(2)}, u32[]{:S(2)}) collective-permute-start(bf16[768,384]{1,0:T(8,128)(2,1)S(1)} %pad_maximum_fusion.2.refs_0_), channel_id=1, source_target_pairs={{0,4},{4,0},{1,5},{5,1},{2,6},{6,2},{3,7},{7,3},{8,12},{12,8},{9,1... | collective-permute-start | bytes 1769480 | tf_op jit(solution)/shard_map/ppermute | solution.py:654
  19.8 35.8 %all-to-all-start = ((bf16[16,192,256]{2,1,0:T(8,128)(2,1)}), bf16[16,192,256]{2,1,0:T(8,128)(2,1)S(1)}, u32[]{:S(2)}, u32[]{:S(2)}) async-start(bf16[16,192,256]{2,1,0:T(8,128)(2,1)} %bitcast.18), calls=%async_computation | async-start | bytes 3145728 | tf_op jit(solution)/shard_map/all_to_all | solution.py:666
  23.7 27.1 %collective-permute-start.4 = (bf16[768,384]{1,0:T(8,128)(2,1)S(1)}, bf16[768,384]{1,0:T(8,128)(2,1)S(1)}, u32[]{:S(2)}, u32[]{:S(2)}) collective-permute-start(bf16[768,384]{1,0:T(8,128)(2,1)S(1)} %pad_maximum_fusion.2.refs_0_), channel_id=1, source_target_pairs={{0,1},{1,0},{2,3},{3,2},{4,5},{5,4},{6,7},{7,6},{8,9},{9,8},{10,11... | collective-permute-start | bytes 1769480 | tf_op jit(solution)/shard_map/ppermute | solution.py:660
  24.2 31.4 %collective-permute-start.5 = (bf16[768,384]{1,0:T(8,128)(2,1)}, bf16[768,384]{1,0:T(8,128)(2,1)}, u32[]{:S(2)}, u32[]{:S(2)}) collective-permute-start(bf16[768,384]{1,0:T(8,128)(2,1)} %collective-permute-done.1.refs_2_), channel_id=1, source_target_pairs={{0,1},{1,0},{2,3},{3,2},{4,5},{5,4},{6,7},{7,6},{8,9},{9,8},{10,11... | collective-permute-start | bytes 1769480 | tf_op jit(solution)/shard_map/ppermute | solution.py:660
  24.3 31.3 %collective-permute-start.6 = (bf16[768,384]{1,0:T(8,128)(2,1)}, bf16[768,384]{1,0:T(8,128)(2,1)}, u32[]{:S(2)}, u32[]{:S(2)}) collective-permute-start(bf16[768,384]{1,0:T(8,128)(2,1)} %collective-permute-done.refs_4_), channel_id=1, source_target_pairs={{0,1},{1,0},{2,3},{3,2},{4,5},{5,4},{6,7},{7,6},{8,9},{9,8},{10,11... | collective-permute-start | bytes 1769480 | tf_op jit(solution)/shard_map/ppermute | solution.py:660
  24.7 17.9 %collective-permute-start.7 = (f32[96,128]{1,0:T(8,128)S(1)}, f32[96,128]{1,0:T(8,128)S(1)}, u32[]{:S(2)}, u32[]{:S(2)}) collective-permute-start(f32[96,128]{1,0:T(8,128)S(1)} %pad_bitcast_fusion), channel_id=1, source_target_pairs={{0,2},{1,3},{2,0},{3,1},{4,6},{5,7},{6,4},{7,5},{8,10},{9,11},{10,... | collective-permute-start | bytes 147464 | tf_op jit(solution)/shard_map/ppermute | solution.py:657
  26.4 21.8 %collective-permute-start.8 = (f32[96,128]{1,0:T(8,128)S(1)}, f32[96,128]{1,0:T(8,128)S(1)}, u32[]{:S(2)}, u32[]{:S(2)}) collective-permute-start(f32[96,128]{1,0:T(8,128)S(1)} %pad_bitcast_fusion), channel_id=1, source_target_pairs={{0,4},{4,0},{1,5},{5,1},{2,6},{6,2},{3,7},{7,3},{8,12},{12,8},{9,1... | collective-permute-start | bytes 147464 | tf_op jit(solution)/shard_map/ppermute | solution.py:654
  56.3 24.2 %collective-permute-start.17 = (bf16[384,768]{1,0:T(8,128)(2,1)}, bf16[384,768]{1,0:T(8,128)(2,1)S(1)}, u32[]{:S(2)}, u32[]{:S(2)}) collective-permute-start(bf16[384,768]{1,0:T(8,128)(2,1)} %refs_0_.2), channel_id=1, source_target_pairs={{0,1},{1,0},{2,3},{3,2},{4,5},{5,4},{6,7},{7,6},{8,9},{9,8},{10,11... | collective-permute-start | bytes 1769480 | tf_op jit(solution)/shard_map/ppermute | solution.py:660
  56.5 15.8 %collective-permute-start.14 = (bf16[384,768]{1,0:T(8,128)(2,1)}, bf16[384,768]{1,0:T(8,128)(2,1)S(1)}, u32[]{:S(2)}, u32[]{:S(2)}) collective-permute-start(bf16[384,768]{1,0:T(8,128)(2,1)} %refs_0_.2), channel_id=1, source_target_pairs={{0,2},{1,3},{2,0},{3,1},{4,6},{5,7},{6,4},{7,5},{8,10},{9,11},{10,... | collective-permute-start | bytes 1769480 | tf_op jit(solution)/shard_map/ppermute | solution.py:657
  57.9 15.6 %collective-permute-start.13 = (bf16[384,768]{1,0:T(8,128)(2,1)}, bf16[384,768]{1,0:T(8,128)(2,1)S(1)}, u32[]{:S(2)}, u32[]{:S(2)}) collective-permute-start(bf16[384,768]{1,0:T(8,128)(2,1)} %refs_0_.2), channel_id=1, source_target_pairs={{0,4},{4,0},{1,5},{5,1},{2,6},{6,2},{3,7},{7,3},{8,12},{12,8},{9,1... | collective-permute-start | bytes 1769480 | tf_op jit(solution)/shard_map/ppermute | solution.py:654
  84.2 23.5 %collective-permute-start.26 = (bf16[768,384]{1,0:T(8,128)(2,1)S(1)}, bf16[768,384]{1,0:T(8,128)(2,1)S(1)}, u32[]{:S(2)}, u32[]{:S(2)}) collective-permute-start(bf16[768,384]{1,0:T(8,128)(2,1)S(1)} %copy-done.38), channel_id=1, source_target_pairs={{0,1},{1,0},{2,3},{3,2},{4,5},{5,4},{6,7},{7,6},{8,9},{9,8},{10,11... | collective-permute-start | bytes 1769480 | tf_op jit(solution)/shard_map/ppermute | solution.py:660
  84.3 15.7 %collective-permute-start.23 = (bf16[768,384]{1,0:T(8,128)(2,1)S(1)}, bf16[768,384]{1,0:T(8,128)(2,1)S(1)}, u32[]{:S(2)}, u32[]{:S(2)}) collective-permute-start(bf16[768,384]{1,0:T(8,128)(2,1)S(1)} %copy-done.38), channel_id=1, source_target_pairs={{0,2},{1,3},{2,0},{3,1},{4,6},{5,7},{6,4},{7,5},{8,10},{9,11},{10,... | collective-permute-start | bytes 1769480 | tf_op jit(solution)/shard_map/ppermute | solution.py:657
  85.5 15.4 %collective-permute-start.22 = (bf16[768,384]{1,0:T(8,128)(2,1)S(1)}, bf16[768,384]{1,0:T(8,128)(2,1)S(1)}, u32[]{:S(2)}, u32[]{:S(2)}) collective-permute-start(bf16[768,384]{1,0:T(8,128)(2,1)S(1)} %copy-done.38), channel_id=1, source_target_pairs={{0,4},{4,0},{1,5},{5,1},{2,6},{6,2},{3,7},{7,3},{8,12},{12,8},{9,1... | collective-permute-start | bytes 1769480 | tf_op jit(solution)/shard_map/ppermute | solution.py:654
  100.9 10.2 %collective-permute-start.27 = (bf16[768,384]{1,0:T(8,128)(2,1)S(1)}, bf16[768,384]{1,0:T(8,128)(2,1)S(1)}, u32[]{:S(2)}, u32[]{:S(2)}) collective-permute-start(bf16[768,384]{1,0:T(8,128)(2,1)S(1)} %collective-permute-done.23.refs_2_), channel_id=1, source_target_pairs={{0,1},{1,0},{2,3},{3,2},{4,5},{5,4},{6,7},{7,6},{8,9},{9,8},{10,11... | collective-permute-start | bytes 1769480 | tf_op jit(solution)/shard_map/ppermute | solution.py:660
  127.6 19.3 %collective-permute-start.32 = (bf16[2,384,384]{2,1,0:T(8,128)(2,1)S(1)}, bf16[2,384,384]{2,1,0:T(8,128)(2,1)S(1)}, u32[]{:S(2)}, u32[]{:S(2)}) collective-permute-start(bf16[2,384,384]{2,1,0:T(8,128)(2,1)S(1)} %get-tuple-element.176), channel_id=1, source_target_pairs={{0,4},{4,0},{1,5},{5,1},{2,6},{6,2},{3,7},{7,3},{8,12},{12,8},{9,1... | collective-permute-start | bytes 1769480 | tf_op jit(solution)/shard_map/ppermute | solution.py:654
  129.4 17.5 %collective-permute-start.33 = (bf16[2,384,384]{2,1,0:T(8,128)(2,1)S(1)}, bf16[2,384,384]{2,1,0:T(8,128)(2,1)S(1)}, u32[]{:S(2)}, u32[]{:S(2)}) collective-permute-start(bf16[2,384,384]{2,1,0:T(8,128)(2,1)S(1)} %get-tuple-element.177), channel_id=1, source_target_pairs={{0,2},{1,3},{2,0},{3,1},{4,6},{5,7},{6,4},{7,5},{8,10},{9,11},{10,... | collective-permute-start | bytes 1769480 | tf_op jit(solution)/shard_map/ppermute | solution.py:657
  150.0 16.6 %collective-permute-start.36 = (bf16[384,384]{1,0:T(8,128)(2,1)S(1)}, bf16[384,384]{1,0:T(8,128)(2,1)S(1)}, u32[]{:S(2)}, u32[]{:S(2)}) collective-permute-start(bf16[384,384]{1,0:T(8,128)(2,1)S(1)} %slice_bitcast_fusion.7), channel_id=1, source_target_pairs={{0,4},{4,0},{1,5},{5,1},{2,6},{6,2},{3,7},{7,3},{8,12},{12,8},{9,1... | collective-permute-start | bytes 884744 | tf_op jit(solution)/shard_map/ppermute | solution.py:654
  152.5 14.2 %collective-permute-start.35 = (bf16[384,384]{1,0:T(8,128)(2,1)S(1)}, bf16[384,384]{1,0:T(8,128)(2,1)S(1)}, u32[]{:S(2)}, u32[]{:S(2)}) collective-permute-start(bf16[384,384]{1,0:T(8,128)(2,1)S(1)} %slice_bitcast_fusion.8), channel_id=1, source_target_pairs={{0,2},{1,3},{2,0},{3,1},{4,6},{5,7},{6,4},{7,5},{8,10},{9,11},{10,... | collective-permute-start | bytes 884744 | tf_op jit(solution)/shard_map/ppermute | solution.py:657
  169.1 18.3 %collective-permute-start.38 = (bf16[2,480,384]{2,1,0:T(8,128)(2,1)S(1)}, bf16[2,480,384]{2,1,0:T(8,128)(2,1)S(1)}, u32[]{:S(2)}, u32[]{:S(2)}) collective-permute-start(bf16[2,480,384]{2,1,0:T(8,128)(2,1)S(1)} %get-tuple-element.203), channel_id=1, source_target_pairs={{0,4},{4,0},{1,5},{5,1},{2,6},{6,2},{3,7},{7,3},{8,12},{12,8},{9,1... | collective-permute-start | bytes 2211848 | tf_op jit(solution)/shard_map/ppermute | solution.py:654
  169.6 18.0 %collective-permute-start.39 = (bf16[2,480,384]{2,1,0:T(8,128)(2,1)S(1)}, bf16[2,480,384]{2,1,0:T(8,128)(2,1)S(1)}, u32[]{:S(2)}, u32[]{:S(2)}) collective-permute-start(bf16[2,480,384]{2,1,0:T(8,128)(2,1)S(1)} %get-tuple-element.204), channel_id=1, source_target_pairs={{0,2},{1,3},{2,0},{3,1},{4,6},{5,7},{6,4},{7,5},{8,10},{9,11},{10,... | collective-permute-start | bytes 2211848 | tf_op jit(solution)/shard_map/ppermute | solution.py:657
  176.5 20.1 %collective-permute-start.40 = (bf16[384,384]{1,0:T(8,128)(2,1)S(1)}, bf16[384,384]{1,0:T(8,128)(2,1)S(1)}, u32[]{:S(2)}, u32[]{:S(2)}) collective-permute-start(bf16[384,384]{1,0:T(8,128)(2,1)S(1)} %select_add_fusion.1), channel_id=1, source_target_pairs={{0,16},{8,24},{16,0},{24,8},{1,17},{9,25},{17,1},{25,9},{2,18},{10... | collective-permute-start | bytes 884744 | tf_op jit(solution)/shard_map/ppermute | solution.py:663
  198.6 12.4 %collective-permute-start.45 = (bf16[384,384]{1,0:T(8,128)(2,1)S(1)}, bf16[384,384]{1,0:T(8,128)(2,1)S(1)}, u32[]{:S(2)}, u32[]{:S(2)}) collective-permute-start(bf16[384,384]{1,0:T(8,128)(2,1)S(1)} %add.132), channel_id=1, source_target_pairs={{0,8},{8,0},{16,24},{24,16},{1,9},{9,1},{17,25},{25,17},{2,10},{10... | collective-permute-start | bytes 884744 | tf_op jit(solution)/shard_map/ppermute | solution.py:663
  199.8 16.2 %collective-permute-start.44 = (bf16[480,384]{1,0:T(8,128)(2,1)S(1)}, bf16[480,384]{1,0:T(8,128)(2,1)S(1)}, u32[]{:S(2)}, u32[]{:S(2)}) collective-permute-start(bf16[480,384]{1,0:T(8,128)(2,1)S(1)} %broadcast_select_fusion.2), channel_id=1, source_target_pairs={{0,8},{8,0},{16,24},{24,16},{1,9},{9,1},{17,25},{25,17},{2,10},{10... | collective-permute-start | bytes 1105928 | tf_op jit(solution)/shard_map/ppermute | solution.py:663
  202.6 13.6 %collective-permute-start.46 = (bf16[2,304,384]{2,1,0:T(8,128)(2,1)S(1)}, bf16[2,304,384]{2,1,0:T(8,128)(2,1)S(1)}, u32[]{:S(2)}, u32[]{:S(2)}) collective-permute-start(bf16[2,304,384]{2,1,0:T(8,128)(2,1)S(1)} %fusion.4), channel_id=1, source_target_pairs={{0,4},{4,0},{1,5},{5,1},{2,6},{6,2},{3,7},{7,3},{8,12},{12,8},{9,1... | collective-permute-start | bytes 1400840 | tf_op jit(solution)/shard_map/ppermute | solution.py:654
  203.7 12.5 %collective-permute-start.47 = (bf16[2,304,384]{2,1,0:T(8,128)(2,1)S(1)}, bf16[2,304,384]{2,1,0:T(8,128)(2,1)S(1)}, u32[]{:S(2)}, u32[]{:S(2)}) collective-permute-start(bf16[2,304,384]{2,1,0:T(8,128)(2,1)S(1)} %fusion.3), channel_id=1, source_target_pairs={{0,2},{1,3},{2,0},{3,1},{4,6},{5,7},{6,4},{7,5},{8,10},{9,11},{10,... | collective-permute-start | bytes 1400840 | tf_op jit(solution)/shard_map/ppermute | solution.py:657
  218.2 18.6 %collective-permute-start.51 = (bf16[480,384]{1,0:T(8,128)(2,1)S(1)}, bf16[480,384]{1,0:T(8,128)(2,1)S(1)}, u32[]{:S(2)}, u32[]{:S(2)}) collective-permute-start(bf16[480,384]{1,0:T(8,128)(2,1)S(1)} %select_add_fusion), channel_id=1, source_target_pairs={{0,16},{8,24},{16,0},{24,8},{1,17},{9,25},{17,1},{25,9},{2,18},{10... | collective-permute-start | bytes 1105928 | tf_op jit(solution)/shard_map/ppermute | solution.py:663
  225.0 14.8 %collective-permute-start.50 = (bf16[304,384]{1,0:T(8,128)(2,1)}, bf16[304,384]{1,0:T(8,128)(2,1)}, u32[]{:S(2)}, u32[]{:S(2)}) collective-permute-start(bf16[304,384]{1,0:T(8,128)(2,1)} %broadcast_select_fusion.8), channel_id=1, source_target_pairs={{0,8},{8,0},{16,24},{24,16},{1,9},{9,1},{17,25},{25,17},{2,10},{10... | collective-permute-start | bytes 700424 | tf_op jit(solution)/shard_map/ppermute | solution.py:663
  225.8 39.2 %all-to-all-start.2 = ((bf16[16,96,256]{2,1,0:T(8,128)(2,1)}), bf16[16,96,256]{2,1,0:T(8,128)(2,1)S(1)}, u32[]{:S(2)}, u32[]{:S(2)}) async-start(bf16[16,96,256]{2,1,0:T(8,128)(2,1)} %bitcast.44), calls=%async_computation.2 | async-start | bytes 1572864 | tf_op jit(solution)/shard_map/all_to_all | solution.py:666
  242.0 19.0 %collective-permute-start.54 = (bf16[480,384]{1,0:T(8,128)(2,1)S(1)}, bf16[480,384]{1,0:T(8,128)(2,1)S(1)}, u32[]{:S(2)}, u32[]{:S(2)}) collective-permute-start(bf16[480,384]{1,0:T(8,128)(2,1)S(1)} %add.142), channel_id=1, source_target_pairs={{0,8},{8,0},{16,24},{24,16},{1,9},{9,1},{17,25},{25,17},{2,10},{10... | collective-permute-start | bytes 1105928 | tf_op jit(solution)/shard_map/ppermute | solution.py:663
  250.8 13.7 %collective-permute-start.53 = (bf16[304,384]{1,0:T(8,128)(2,1)S(1)}, bf16[304,384]{1,0:T(8,128)(2,1)S(1)}, u32[]{:S(2)}, u32[]{:S(2)}) collective-permute-start(bf16[304,384]{1,0:T(8,128)(2,1)S(1)} %add.141), channel_id=1, source_target_pairs={{0,8},{8,0},{16,24},{24,16},{1,9},{9,1},{17,25},{25,17},{2,10},{10... | collective-permute-start | bytes 700424 | tf_op jit(solution)/shard_map/ppermute | solution.py:663
  265.0 17.1 %all-to-all-start.1 = ((bf16[16,96,256]{2,1,0:T(8,128)(2,1)}), bf16[16,96,256]{2,1,0:T(8,128)(2,1)S(1)}, u32[]{:S(2)}, u32[]{:S(2)}) async-start(bf16[16,96,256]{2,1,0:T(8,128)(2,1)} %bitcast.42), calls=%async_computation.1 | async-start | bytes 1572864 | tf_op jit(solution)/shard_map/all_to_all | solution.py:666
  (83 other events, 591.0 us)
where the time goes:
time: 284 us; the launch traced here: 283 us
  Pallas kernels  90.4 us (32%)
  waiting for transfers between devices  82.5 us (29%)
  starting transfers between devices  64.4 us (23%)
  local copies, waits for them, and re-layouts  28.6 us (10%)
  other arithmetic  13.4 us (5%)
  between operations  3.64 us (1%)
    pallas_call x12, Pallas kernels, run(): pl.pallas_call(kernel, out_shape=places[0] if single else tuple(places),...  90.4 us
    ppermute x9, waiting for transfers between devices, flip_dp(): return lax.ppermute(v, 'dp', [(i, i ^ step) for i in range(holders)])  36.1 us
    ppermute x13, waiting for transfers between devices, flip_chip(): return lax.ppermute(v, 'col', [(i, i ^ 2) for i in range(nc)])  29 us
    ppermute x14, starting transfers between devices, flip_row(): return lax.ppermute(v, 'row', [(i, i ^ 1) for i in range(nr)])  21.2 us
    ppermute x9, starting transfers between devices, flip_dp(): return lax.ppermute(v, 'dp', [(i, i ^ step) for i in range(holders)])  14.4 us
    ppermute x13, starting transfers between devices, flip_chip(): return lax.ppermute(v, 'col', [(i, i ^ 2) for i in range(nc)])  13.3 us
    unnamed x115, local copies, waits for them, and re-layouts  11.7 us
    all_to_all x3, starting transfers between devices, exchange(): lax.all_to_all(v, ('dp',) + RC, 0, 0, axis_index_groups=groups, tiled=True)  11.4 us
  transfers between devices with their start and end apart: 58, of which 29 were waited for; matrix products, arithmetic and copies ran while one was open for 10% of the time, Pallas kernels for 28%

commit v1 on v0

--- a/solution.py
+++ b/solution.py
@@ -357,6 +357,12 @@
         r, c = j // 2, j % 2
         outs[r][c] = (up(left[r, c, :h]) + up(right[r, c, :h])).astype(bf16)
         outs[2 + c][r] = (up(left[r, c, h:]) + up(right[r, c, h:])).astype(bf16)
+
+
+def sum_near_kernel(row_own, row_got, chip_own, chip_got, p0, p1, q0, q1):
+    for own, got, outs in ((row_own, row_got, (p0, p1)), (chip_own, chip_got, (q0, q1))):
+        for i in range(2):
+            outs[i][...] = (up(own[i]) + up(got[i])).astype(bf16)
 
 
 def hidden_back_kernel(nc, rw, fw, info, st_ref, e2_ref, pf, left, right, vh_in, slope_in, *refs):
@@ -815,9 +821,12 @@
     def reduce_near(v):
         return flip_row(v[1]), flip_chip(v[3])
 
-    def reduce_far(v, got):
-        p, q = v[0] + got[0], v[2] + got[1]
-        return (p[0], q[0]), (flip_chip(p[1]), flip_row(q[1]))
+    def reduce_far(v, got, name):
+        one = sds(v[0].shape[1:], bf16)
+        p0, p1, q0, q1 = call(
+            sum_near_kernel, (one, one, one, one), [VMEM] * 4, [VMEM] * 4, **time_us(2), name=name
+        )(v[0], got[0], v[2], got[1])
+        return (p0, q0), (flip_chip(p1), flip_row(q1))
 
     def reduce_dp(v, got):
         p, q = v[0] + got[0], v[1] + got[1]
@@ -857,7 +866,7 @@
 
     e1, mid_send, shr_near = tie(e1, mid_send, shr_near)
     mid_got = flip_core(mid_send)
-    shr_stay, shr_far = reduce_far(shr, shr_near)
+    shr_stay, shr_far = reduce_far(shr, shr_near, "shrink_sum")
 
     all_heads = (nc * 3 * hw, unit)
     dqkv, gd_mix, gh, do, qkv, *mid = call(
@@ -896,7 +905,8 @@
     )(info, dqkv, x, dx1, pd, *g1)
 
     gd_in, mid_near = tie(gd_in, mid_near)
-    mid_stay, mid_far = reduce_far(mid, mid_near)
+    p, q = mid[0] + mid_near[0], mid[2] + mid_near[1]
+    mid_stay, mid_far = (p[0], q[0]), (flip_chip(p[1]), flip_row(q[1]))
 
     rows1 = 3 * hw + fl // 3
     part1 = (nr, nc // 2, rows1, rw)

time: 284 us -> 281 us (0.989)
    pallas_call x12 -> x13, Pallas kernels: 90.4 us -> 89.5 us  [run(): pl.pallas_call(kernel, out_shape=places[0] if single else tuple(places),...]
    unnamed x115 -> x129, local copies, waits for them, and re-layouts: 11.7 us -> 12.1 us
  transfers between devices with their start and end apart: 58 -> 58, of which waited for: 29 -> 29; matrix products, arithmetic and copies ran while one was open for 10% -> 9% of each run, Pallas kernels for 28% -> 28%
where the time goes in v1:
time: 281 us; the launch traced here: 280 us
  Pallas kernels  89.5 us (32%)
  waiting for transfers between devices  81.8 us (29%)
  starting transfers between devices  64.9 us (23%)
  local copies, waits for them, and re-layouts  29 us (10%)
  other arithmetic  10.8 us (4%)
  between operations  3.68 us (1%)
    pallas_call x13, Pallas kernels, run(): pl.pallas_call(kernel, out_shape=places[0] if single else tuple(places),...  89.5 us
    ppermute x9, waiting for transfers between devices, flip_dp(): return lax.ppermute(v, 'dp', [(i, i ^ step) for i in range(holders)])  35.9 us
    ppermute x13, waiting for transfers between devices, flip_chip(): return lax.ppermute(v, 'col', [(i, i ^ 2) for i in range(nc)])  29 us
    ppermute x14, starting transfers between devices, flip_row(): return lax.ppermute(v, 'row', [(i, i ^ 1) for i in range(nr)])  20.2 us
    ppermute x13, starting transfers between devices, flip_chip(): return lax.ppermute(v, 'col', [(i, i ^ 2) for i in range(nc)])  14.8 us
    ppermute x9, starting transfers between devices, flip_dp(): return lax.ppermute(v, 'dp', [(i, i ^ step) for i in range(holders)])  14.4 us
    unnamed x129, local copies, waits for them, and re-layouts  12.1 us
    all_to_all x3, starting transfers between devices, exchange(): lax.all_to_all(v, ('dp',) + RC, 0, 0, axis_index_groups=groups, tiled=True)  11.3 us
  transfers between devices with their start and end apart: 58, of which 29 were waited for; matrix products, arithmetic and copies ran while one was open for 9% of the time, Pallas kernels for 28%

profile of v1, /device:TPU:0, one launch (start us, length us, event | category | flops | bytes accessed | tf_op | source)
XLA Modules:
  0.0 279.6 jit_solution(16580264374652621827)
XLA Ops:
  1.9 3.0 %collective-permute-start.1 = (bf16[768,384]{1,0:T(8,128)(2,1)S(1)}, bf16[768,384]{1,0:T(8,128)(2,1)}, u32[]{:S(2)}, u32[]{:S(2)}) collective-permute-start(bf16[768,384]{1,0:T(8,128)(2,1)S(1)} %pad_maximum_fusion.2.refs_0_), channel_id=1, source_target_pairs={{0,2},{1,3},{2,0},{3,1},{4,6},{5,7},{6,4},{7,5},{8,10},{9,11},{10,... | collective-permute-start | bytes 1769480 | tf_op jit(solution)/shard_map/ppermute | solution.py:663
  15.2 3.1 %collective-permute-done.1.refs_2_ = bf16[768,384]{1,0:T(8,128)(2,1)} collective-permute-done((bf16[768,384]{1,0:T(8,128)(2,1)S(1)}, bf16[768,384]{1,0:T(8,128)(2,1)}, u32[]{:S(2)}, u32[]{:S(2)}) %collective-permute-start.1) | collective-permute-done | bytes 589856 | tf_op jit(solution)/shard_map/ppermute | solution.py:663
  19.8 3.9 %all-to-all-start = ((bf16[16,192,256]{2,1,0:T(8,128)(2,1)}), bf16[16,192,256]{2,1,0:T(8,128)(2,1)S(1)}, u32[]{:S(2)}, u32[]{:S(2)}) async-start(bf16[16,192,256]{2,1,0:T(8,128)(2,1)} %bitcast.18), calls=%async_computation | async-start | bytes 3145728 | tf_op jit(solution)/shard_map/all_to_all | solution.py:672
  27.9 14.8 %collective-permute-done.7 = f32[96,128]{1,0:T(8,128)S(1)} collective-permute-done((f32[96,128]{1,0:T(8,128)S(1)}, f32[96,128]{1,0:T(8,128)S(1)}, u32[]{:S(2)}, u32[]{:S(2)}) %collective-permute-start.7) | collective-permute-done | bytes 49184 | tf_op jit(solution)/shard_map/ppermute | solution.py:663
  42.7 3.6 %collective-permute-start.9 = (f32[96,128]{1,0:T(8,128)S(1)}, f32[96,128]{1,0:T(8,128)S(1)}, u32[]{:S(2)}, u32[]{:S(2)}) collective-permute-start(f32[96,128]{1,0:T(8,128)S(1)} %collective-permute-done.7), channel_id=1, source_target_pairs={{0,4},{4,0},{1,5},{5,1},{2,6},{6,2},{3,7},{7,3},{8,12},{12,8},{9,1... | collective-permute-start | bytes 147464 | tf_op jit(solution)/shard_map/ppermute | solution.py:660
  59.9 11.9 %attend.1 = (bf16[768,512]{1,0:T(8,128)(2,1)S(1)}, bf16[768,512]{1,0:T(8,128)(2,1)S(1)}, bf16[4,576,512]{2,1,0:T(8,128)(2,1)}, f32[4,8,512]{2,1,0:T(8,128)S(1)},...) custom-call(s32[5]{0:T(128)S(1)} %pad_add_fusion.info, ...), custom_call_target="tpu_custom_call" | custom-call | flops 12999999488 | bytes 13000000 | tf_op jit(solution)/shard_map/attend/pallas_call | solution.py:141
  76.7 3.8 %output.1 = (bf16[768,512]{1,0:T(8,128)(2,1)S(1)}, f32[768,512]{1,0:T(8,128)S(1)}, bf16[768,512]{1,0:T(8,128)(2,1)S(1)}) custom-call(s32[5]{0:T(128)S(1)} %pad_add_fusion.info, bf16[768,512]{1,0:T(8,128)(2,1)S(1)} %get-tuple-element.146.x_ref, f32[768,512]{1,0:T(8,128)S(1)} %get-tuple-element.145.o_ref, f32[768,16]{1,0:T(8,128)S(1)} %get-tuple-element.147.pd, ...), custom_call_target="tpu_custom_call" | custom-call | flops 5000000000 | bytes 5000000 | tf_op jit(solution)/shard_map/output/pallas_call | solution.py:141
  80.5 2.5 collective-permute-done.16.refs_7_
  87.2 11.6 %expand.1 = (bf16[4,768,512]{2,1,0:T(8,128)(2,1)S(1)}, bf16[4,768,512]{2,1,0:T(8,128)(2,1)}, bf16[4,768,512]{2,1,0:T(8,128)(2,1)}, f32[8,512]{1,0:T(8,128)S(1)}) custom-call(s32[5]{0:T(128)S(1)} %pad_add_fusion.info, bf16[768,512]{1,0:T(8,128)(2,1)S(1)} %get-tuple-element.151.b_ref, f32[4,768,8]{2,1,0:T(8,128)S(1)} %get-tuple-element.152.pf, ...), custom_call_target="tpu_custom_call" | custom-call | flops 12999999488 | bytes 13000000 | tf_op jit(solution)/shard_map/expand/pallas_call | solution.py:141
  104.1 3.5 %shrink_grads.1 = (bf16[768,512]{1,0:T(8,128)(2,1)S(1)}, bf16[2,2,768,384]{3,2,1,0:T(8,128)(2,1)S(1)}, bf16[2,2,768,384]{3,2,1,0:T(8,128)(2,1)S(1)}) custom-call(s32[5]{0:T(128)S(1)} %pad_add_fusion.info, bf16[4,768,512]{2,1,0:T(8,128)(2,1)S(1)} %get-tuple-element.228.gn_ref, bf16[2,8,192,256]{3,2,1,0:T(8,128)(2,1)S(1)} %bitcast.111), custom_call_target="tpu_custom_call" | custom-call | flops 7000000000 | bytes 7000000 | tf_op jit(solution)/shard_map/shrink_grads/pallas_call | solution.py:141
  107.7 2.9 %collective-permute-done.25.refs_7_ = bf16[384,384]{1,0:T(8,128)(2,1)S(1)} collective-permute-done((bf16[384,384]{1,0:T(8,128)(2,1)S(1)}, bf16[384,384]{1,0:T(8,128)(2,1)S(1)}, u32[]{:S(2)}, u32[]{:S(2)}) %collective-permute-start.25) | collective-permute-done | bytes 294944 | tf_op jit(solution)/shard_map/ppermute | solution.py:663
  111.8 4.4 %collective-permute-done.30.refs_8_ = bf16[384,384]{1,0:T(8,128)(2,1)S(1)} collective-permute-done((bf16[384,384]{1,0:T(8,128)(2,1)S(1)}, bf16[384,384]{1,0:T(8,128)(2,1)S(1)}, u32[]{:S(2)}, u32[]{:S(2)}) %collective-permute-start.30) | collective-permute-done | bytes 294944 | tf_op jit(solution)/shard_map/ppermute | solution.py:666
  117.3 10.3 %hidden_back.1 = (bf16[4,768,512]{2,1,0:T(8,128)(2,1)S(1)}, f32[4,768,8]{2,1,0:T(8,128)S(1)}, bf16[2,384,384]{2,1,0:T(8,128)(2,1)S(1)}, bf16[2,384,384]{2,1,0:T(...) custom-call(s32[5]{0:T(128)S(1)} %pad_add_fusion.info, ...), custom_call_target="tpu_custom_call" | custom-call | flops 12999999488 | bytes 13000000 | tf_op jit(solution)/shard_map/hidden_back/pallas_call | solution.py:141
  129.8 7.5 %middle_back.1 = (f32[768,512]{1,0:T(8,128)S(1)}, bf16[768,512]{1,0:T(8,128)(2,1)S(1)}, f32[768,8]{1,0:T(8,128)S(1)}) custom-call(s32[5]{0:T(128)S(1)} %pad_add_fusion.info, bf16[4,768,512]{2,1,0:T(8,128)(2,1)S(1)} %get-tuple-element.175.df_ref, f32[768,512]{1,0:T(8,128)S(1)} %get-tuple-element.176.x1_ref, bf16[768,512]{1,0:T(8,128)(2,1)S(1)} %get-tuple-element.162.e2_ref, ...), custom_call_target="tpu_custom_call" | custom-call | flops 8000000000 | bytes 8000000 | tf_op jit(solution)/shard_map/middle_back/pallas_call | solution.py:141
  139.3 6.0 %middle_grads.1 = (bf16[2,2,960,384]{3,2,1,0:T(8,128)(2,1)S(1)}, bf16[2,2,960,384]{3,2,1,0:T(8,128)(2,1)}) custom-call(s32[5]{0:T(128)S(1)} %pad_add_fusion.info, bf16[768,512]{1,0:T(8,128)(2,1)S(1)} %get-tuple-element.151.b_ref, bf16[4,768,512]{2,1,0:T(8,128)(2,1)S(1)} %get-tuple-element.175.df_ref, bf16[4,192,512]{2,1,0:T(8,128)(2,1)S(1)} %bitcast.113, ...), custom_call_target="tpu_custom_call" | custom-call | flops 7000000000 | bytes 7000000 | tf_op jit(solution)/shard_map/middle_grads/pallas_call | solution.py:141
  153.6 8.9 %attend_back.1 = (bf16[2304,512]{1,0:T(8,128)(2,1)S(1)}, f32[768,8]{1,0:T(8,128)S(1)}, f32[4,192,8]{2,1,0:T(8,128)S(1)}, bf16[768,512]{1,0:T(8,128)(2,1)S(1)}, b...) custom-call(s32[5]{0:T(128)S(1)} %pad_add_fusion.info, ...), custom_call_target="tpu_custom_call" | custom-call | flops 11000000512 | bytes 11000000 | tf_op jit(solution)/shard_map/attend_back/pallas_call | solution.py:141
  166.8 4.8 %attend_back_rest.1 = (bf16[2304,512]{1,0:T(8,128)(2,1)S(1)}, f32[4,192,8]{2,1,0:T(8,128)S(1)}) custom-call(s32[5]{0:T(128)S(1)} %pad_add_fusion.info, f32[768,512]{1,0:T(8,128)S(1)} %copy-done.13, bf16[4,576,512]{2,1,0:T(8,128)(2,1)S(1)} %get-tuple-element.187.qkv_ref, f32[4,8,512]{2,1,0:T(8,128)S(1)} %copy-done.31, ...), custom_call_target="tpu_custom_call", output_to_operand_aliasing={{0}: (5, {}), {1}: (6, {})} | custom-call | flops 8000000000 | bytes 8000000 | tf_op jit(solution)/shard_map/attend_back_rest/pallas_call | solution.py:141
  172.7 2.6 collective-permute-start.40
  175.4 8.3 %input_back.1 = (bf16[2,768,256]{2,1,0:T(8,128)(2,1)}, f32[768,8]{1,0:T(8,128)S(1)}) custom-call(s32[5]{0:T(128)S(1)} %pad_add_fusion.info, bf16[2304,512]{1,0:T(8,128)(2,1)S(1)} %get-tuple-element.207.dqkv, bf16[768,512]{1,0:T(8,128)(2,1)S(1)} %copy-done.17, f32[768,512]{1,0:T(8,128)S(1)} %copy-done.19, f32[768,16]{1,0:T(8,128)S(1)} %copy-done.23, ...), custom_call_target="tpu_custom_call" | custom-call | flops 7000000000 | bytes 7000000 | tf_op jit(solution)/shard_map/input_back/pallas_call | solution.py:141
  186.6 6.2 %attend_grads.1 = (bf16[2,2,608,384]{3,2,1,0:T(8,128)(2,1)S(1)}, bf16[2,2,608,384]{3,2,1,0:T(8,128)(2,1)S(1)}) custom-call(s32[5]{0:T(128)S(1)} %pad_add_fusion.info, bf16[2304,512]{1,0:T(8,128)(2,1)S(1)} %get-tuple-element.207.dqkv, bf16[768,512]{1,0:T(8,128)(2,1)S(1)} %copy-done.27, f32[768,8]{1,0:T(8,128)S(1)} %get-tuple-element.213.gd_in, ...), custom_call_target="tpu_custom_call" | custom-call | flops 7000000000 | bytes 7000000 | tf_op jit(solution)/shard_map/attend_grads/pallas_call | solution.py:141
  201.1 6.6 %shrink.1 = bf16[2,768,256]{2,1,0:T(8,128)(2,1)} custom-call(s32[5]{0:T(128)S(1)} %pad_add_fusion.info, f32[768,16]{1,0:T(8,128)S(1)} %copy-done.23, bf16[3072,512]{1,0:T(8,128)(2,1)S(1)} %bitcast.112, f32[768,512]{1,0:T(8,128)S(1)} %copy-done.11, bf16[768,384]{1,0:T(8,128)(2,1)} %refs_0_.3, bf16[768,384]{1,0:T(8,128)(2,1)} %copy-done.47, ...), custom_call_target="tpu_custom_call" | custom-call | flops 8000000000 | bytes 8000000 | tf_op jit(solution)/shard_map/shrink/pallas_call | solution.py:141
  207.7 5.0 %collective-permute-done.44 = bf16[480,384]{1,0:T(8,128)(2,1)S(1)} collective-permute-done((bf16[480,384]{1,0:T(8,128)(2,1)S(1)}, bf16[480,384]{1,0:T(8,128)(2,1)S(1)}, u32[]{:S(2)}, u32[]{:S(2)}) %collective-permute-start.44) | collective-permute-done | bytes 368672 | tf_op jit(solution)/shard_map/ppermute | solution.py:669
  217.3 3.1 %collective-permute-done.48 = bf16[304,384]{1,0:T(8,128)(2,1)S(1)} collective-permute-done((bf16[304,384]{1,0:T(8,128)(2,1)S(1)}, bf16[304,384]{1,0:T(8,128)(2,1)S(1)}, u32[]{:S(2)}, u32[]{:S(2)}) %collective-permute-start.48) | collective-permute-done | bytes 233504 | tf_op jit(solution)/shard_map/ppermute | solution.py:663
  222.4 3.8 %all-to-all-start.2 = ((bf16[16,96,256]{2,1,0:T(8,128)(2,1)}), bf16[16,96,256]{2,1,0:T(8,128)(2,1)S(1)}, u32[]{:S(2)}, u32[]{:S(2)}) async-start(bf16[16,96,256]{2,1,0:T(8,128)(2,1)} %bitcast.40), calls=%async_computation.2 | async-start | bytes 1572864 | tf_op jit(solution)/shard_map/all_to_all | solution.py:672
  226.2 7.2 %collective-permute-done.51 = bf16[480,384]{1,0:T(8,128)(2,1)S(1)} collective-permute-done((bf16[480,384]{1,0:T(8,128)(2,1)S(1)}, bf16[480,384]{1,0:T(8,128)(2,1)S(1)}, u32[]{:S(2)}, u32[]{:S(2)}) %collective-permute-start.51) | collective-permute-done | bytes 368672 | tf_op jit(solution)/shard_map/ppermute | solution.py:669
  233.4 2.9 %collective-permute-done.50 = bf16[304,384]{1,0:T(8,128)(2,1)} collective-permute-done((bf16[304,384]{1,0:T(8,128)(2,1)}, bf16[304,384]{1,0:T(8,128)(2,1)}, u32[]{:S(2)}, u32[]{:S(2)}) %collective-permute-start.50) | collective-permute-done | bytes 233504 | tf_op jit(solution)/shard_map/ppermute | solution.py:669
  238.6 2.5 collective-permute-start.54
  241.2 6.2 %collective-permute-done.52 = bf16[304,384]{1,0:T(8,128)(2,1)S(1)} collective-permute-done((bf16[304,384]{1,0:T(8,128)(2,1)S(1)}, bf16[304,384]{1,0:T(8,128)(2,1)S(1)}, u32[]{:S(2)}, u32[]{:S(2)}) %collective-permute-start.52) | collective-permute-done | bytes 233504 | tf_op jit(solution)/shard_map/ppermute | solution.py:669
  247.8 9.9 %collective-permute-done.54 = bf16[480,384]{1,0:T(8,128)(2,1)S(1)} collective-permute-done((bf16[480,384]{1,0:T(8,128)(2,1)S(1)}, bf16[480,384]{1,0:T(8,128)(2,1)S(1)}, u32[]{:S(2)}, u32[]{:S(2)}) %collective-permute-start.54) | collective-permute-done | bytes 368672 | tf_op jit(solution)/shard_map/ppermute | solution.py:669
  257.6 3.6 %collective-permute-done.53 = bf16[304,384]{1,0:T(8,128)(2,1)S(1)} collective-permute-done((bf16[304,384]{1,0:T(8,128)(2,1)S(1)}, bf16[304,384]{1,0:T(8,128)(2,1)S(1)}, u32[]{:S(2)}, u32[]{:S(2)}) %collective-permute-start.53) | collective-permute-done | bytes 233504 | tf_op jit(solution)/shard_map/ppermute | solution.py:669
  261.7 3.6 %all-to-all-start.1 = ((bf16[16,96,256]{2,1,0:T(8,128)(2,1)}), bf16[16,96,256]{2,1,0:T(8,128)(2,1)S(1)}, u32[]{:S(2)}, u32[]{:S(2)}) async-start(bf16[16,96,256]{2,1,0:T(8,128)(2,1)} %bitcast.38), calls=%async_computation.1 | async-start | bytes 1572864 | tf_op jit(solution)/shard_map/all_to_all | solution.py:672
  275.3 3.4 %all-to-all-done.1 = bf16[16,96,256]{2,1,0:T(8,128)(2,1)S(1)} async-done(((bf16[16,96,256]{2,1,0:T(8,128)(2,1)}), bf16[16,96,256]{2,1,0:T(8,128)(2,1)S(1)}, u32[]{:S(2)}, u32[]{:S(2)}) %all-to-all-start.1) | async-done | bytes 786464 | tf_op jit(solution)/shard_map/all_to_all | solution.py:672
  (302 shorter events, 94.5 us)
Async XLA Ops:
  1.9 16.5 %collective-permute-start.1 = (bf16[768,384]{1,0:T(8,128)(2,1)S(1)}, bf16[768,384]{1,0:T(8,128)(2,1)}, u32[]{:S(2)}, u32[]{:S(2)}) collective-permute-start(bf16[768,384]{1,0:T(8,128)(2,1)S(1)} %pad_maximum_fusion.2.refs_0_), channel_id=1, source_target_pairs={{0,2},{1,3},{2,0},{3,1},{4,6},{5,7},{6,4},{7,5},{8,10},{9,11},{10,... | collective-permute-start | bytes 1769480 | tf_op jit(solution)/shard_map/ppermute | solution.py:663
  5.0 14.9 %collective-permute-start = (bf16[768,384]{1,0:T(8,128)(2,1)S(1)}, bf16[768,384]{1,0:T(8,128)(2,1)}, u32[]{:S(2)}, u32[]{:S(2)}) collective-permute-start(bf16[768,384]{1,0:T(8,128)(2,1)S(1)} %pad_maximum_fusion.2.refs_0_), channel_id=1, source_target_pairs={{0,4},{4,0},{1,5},{5,1},{2,6},{6,2},{3,7},{7,3},{8,12},{12,8},{9,1... | collective-permute-start | bytes 1769480 | tf_op jit(solution)/shard_map/ppermute | solution.py:660
  19.8 35.8 %all-to-all-start = ((bf16[16,192,256]{2,1,0:T(8,128)(2,1)}), bf16[16,192,256]{2,1,0:T(8,128)(2,1)S(1)}, u32[]{:S(2)}, u32[]{:S(2)}) async-start(bf16[16,192,256]{2,1,0:T(8,128)(2,1)} %bitcast.18), calls=%async_computation | async-start | bytes 3145728 | tf_op jit(solution)/shard_map/all_to_all | solution.py:672
  23.7 27.1 %collective-permute-start.4 = (bf16[768,384]{1,0:T(8,128)(2,1)S(1)}, bf16[768,384]{1,0:T(8,128)(2,1)S(1)}, u32[]{:S(2)}, u32[]{:S(2)}) collective-permute-start(bf16[768,384]{1,0:T(8,128)(2,1)S(1)} %pad_maximum_fusion.2.refs_0_), channel_id=1, source_target_pairs={{0,1},{1,0},{2,3},{3,2},{4,5},{5,4},{6,7},{7,6},{8,9},{9,8},{10,11... | collective-permute-start | bytes 1769480 | tf_op jit(solution)/shard_map/ppermute | solution.py:666
  24.2 31.4 %collective-permute-start.5 = (bf16[768,384]{1,0:T(8,128)(2,1)}, bf16[768,384]{1,0:T(8,128)(2,1)}, u32[]{:S(2)}, u32[]{:S(2)}) collective-permute-start(bf16[768,384]{1,0:T(8,128)(2,1)} %collective-permute-done.1.refs_2_), channel_id=1, source_target_pairs={{0,1},{1,0},{2,3},{3,2},{4,5},{5,4},{6,7},{7,6},{8,9},{9,8},{10,11... | collective-permute-start | bytes 1769480 | tf_op jit(solution)/shard_map/ppermute | solution.py:666
  24.3 31.3 %collective-permute-start.6 = (bf16[768,384]{1,0:T(8,128)(2,1)}, bf16[768,384]{1,0:T(8,128)(2,1)}, u32[]{:S(2)}, u32[]{:S(2)}) collective-permute-start(bf16[768,384]{1,0:T(8,128)(2,1)} %collective-permute-done.refs_4_), channel_id=1, source_target_pairs={{0,1},{1,0},{2,3},{3,2},{4,5},{5,4},{6,7},{7,6},{8,9},{9,8},{10,11... | collective-permute-start | bytes 1769480 | tf_op jit(solution)/shard_map/ppermute | solution.py:666
  24.7 17.9 %collective-permute-start.7 = (f32[96,128]{1,0:T(8,128)S(1)}, f32[96,128]{1,0:T(8,128)S(1)}, u32[]{:S(2)}, u32[]{:S(2)}) collective-permute-start(f32[96,128]{1,0:T(8,128)S(1)} %pad_bitcast_fusion), channel_id=1, source_target_pairs={{0,2},{1,3},{2,0},{3,1},{4,6},{5,7},{6,4},{7,5},{8,10},{9,11},{10,... | collective-permute-start | bytes 147464 | tf_op jit(solution)/shard_map/ppermute | solution.py:663
  26.4 21.8 %collective-permute-start.8 = (f32[96,128]{1,0:T(8,128)S(1)}, f32[96,128]{1,0:T(8,128)S(1)}, u32[]{:S(2)}, u32[]{:S(2)}) collective-permute-start(f32[96,128]{1,0:T(8,128)S(1)} %pad_bitcast_fusion), channel_id=1, source_target_pairs={{0,4},{4,0},{1,5},{5,1},{2,6},{6,2},{3,7},{7,3},{8,12},{12,8},{9,1... | collective-permute-start | bytes 147464 | tf_op jit(solution)/shard_map/ppermute | solution.py:660
  56.3 24.2 %collective-permute-start.17 = (bf16[384,768]{1,0:T(8,128)(2,1)}, bf16[384,768]{1,0:T(8,128)(2,1)S(1)}, u32[]{:S(2)}, u32[]{:S(2)}) collective-permute-start(bf16[384,768]{1,0:T(8,128)(2,1)} %refs_0_.2), channel_id=1, source_target_pairs={{0,1},{1,0},{2,3},{3,2},{4,5},{5,4},{6,7},{7,6},{8,9},{9,8},{10,11... | collective-permute-start | bytes 1769480 | tf_op jit(solution)/shard_map/ppermute | solution.py:666
  56.5 15.8 %collective-permute-start.14 = (bf16[384,768]{1,0:T(8,128)(2,1)}, bf16[384,768]{1,0:T(8,128)(2,1)S(1)}, u32[]{:S(2)}, u32[]{:S(2)}) collective-permute-start(bf16[384,768]{1,0:T(8,128)(2,1)} %refs_0_.2), channel_id=1, source_target_pairs={{0,2},{1,3},{2,0},{3,1},{4,6},{5,7},{6,4},{7,5},{8,10},{9,11},{10,... | collective-permute-start | bytes 1769480 | tf_op jit(solution)/shard_map/ppermute | solution.py:663
  57.9 15.6 %collective-permute-start.13 = (bf16[384,768]{1,0:T(8,128)(2,1)}, bf16[384,768]{1,0:T(8,128)(2,1)S(1)}, u32[]{:S(2)}, u32[]{:S(2)}) collective-permute-start(bf16[384,768]{1,0:T(8,128)(2,1)} %refs_0_.2), channel_id=1, source_target_pairs={{0,4},{4,0},{1,5},{5,1},{2,6},{6,2},{3,7},{7,3},{8,12},{12,8},{9,1... | collective-permute-start | bytes 1769480 | tf_op jit(solution)/shard_map/ppermute | solution.py:660
  84.2 23.5 %collective-permute-start.26 = (bf16[768,384]{1,0:T(8,128)(2,1)S(1)}, bf16[768,384]{1,0:T(8,128)(2,1)S(1)}, u32[]{:S(2)}, u32[]{:S(2)}) collective-permute-start(bf16[768,384]{1,0:T(8,128)(2,1)S(1)} %copy-done.45), channel_id=1, source_target_pairs={{0,1},{1,0},{2,3},{3,2},{4,5},{5,4},{6,7},{7,6},{8,9},{9,8},{10,11... | collective-permute-start | bytes 1769480 | tf_op jit(solution)/shard_map/ppermute | solution.py:666
  84.3 15.7 %collective-permute-start.23 = (bf16[768,384]{1,0:T(8,128)(2,1)S(1)}, bf16[768,384]{1,0:T(8,128)(2,1)S(1)}, u32[]{:S(2)}, u32[]{:S(2)}) collective-permute-start(bf16[768,384]{1,0:T(8,128)(2,1)S(1)} %copy-done.45), channel_id=1, source_target_pairs={{0,2},{1,3},{2,0},{3,1},{4,6},{5,7},{6,4},{7,5},{8,10},{9,11},{10,... | collective-permute-start | bytes 1769480 | tf_op jit(solution)/shard_map/ppermute | solution.py:663
  85.5 15.4 %collective-permute-start.22 = (bf16[768,384]{1,0:T(8,128)(2,1)S(1)}, bf16[768,384]{1,0:T(8,128)(2,1)S(1)}, u32[]{:S(2)}, u32[]{:S(2)}) collective-permute-start(bf16[768,384]{1,0:T(8,128)(2,1)S(1)} %copy-done.45), channel_id=1, source_target_pairs={{0,4},{4,0},{1,5},{5,1},{2,6},{6,2},{3,7},{7,3},{8,12},{12,8},{9,1... | collective-permute-start | bytes 1769480 | tf_op jit(solution)/shard_map/ppermute | solution.py:660
  100.9 10.2 %collective-permute-start.27 = (bf16[768,384]{1,0:T(8,128)(2,1)S(1)}, bf16[768,384]{1,0:T(8,128)(2,1)S(1)}, u32[]{:S(2)}, u32[]{:S(2)}) collective-permute-start(bf16[768,384]{1,0:T(8,128)(2,1)S(1)} %collective-permute-done.23.refs_2_), channel_id=1, source_target_pairs={{0,1},{1,0},{2,3},{3,2},{4,5},{5,4},{6,7},{7,6},{8,9},{9,8},{10,11... | collective-permute-start | bytes 1769480 | tf_op jit(solution)/shard_map/ppermute | solution.py:666
  101.1 10.1 %collective-permute-start.28 = (bf16[768,384]{1,0:T(8,128)(2,1)S(1)}, bf16[768,384]{1,0:T(8,128)(2,1)S(1)}, u32[]{:S(2)}, u32[]{:S(2)}) collective-permute-start(bf16[768,384]{1,0:T(8,128)(2,1)S(1)} %collective-permute-done.22.refs_4_), channel_id=1, source_target_pairs={{0,1},{1,0},{2,3},{3,2},{4,5},{5,4},{6,7},{7,6},{8,9},{9,8},{10,11... | collective-permute-start | bytes 1769480 | tf_op jit(solution)/shard_map/ppermute | solution.py:666
  127.6 19.3 %collective-permute-start.32 = (bf16[2,384,384]{2,1,0:T(8,128)(2,1)S(1)}, bf16[2,384,384]{2,1,0:T(8,128)(2,1)S(1)}, u32[]{:S(2)}, u32[]{:S(2)}) collective-permute-start(bf16[2,384,384]{2,1,0:T(8,128)(2,1)S(1)} %get-tuple-element.180), channel_id=1, source_target_pairs={{0,4},{4,0},{1,5},{5,1},{2,6},{6,2},{3,7},{7,3},{8,12},{12,8},{9,1... | collective-permute-start | bytes 1769480 | tf_op jit(solution)/shard_map/ppermute | solution.py:660
  129.4 17.5 %collective-permute-start.33 = (bf16[2,384,384]{2,1,0:T(8,128)(2,1)S(1)}, bf16[2,384,384]{2,1,0:T(8,128)(2,1)S(1)}, u32[]{:S(2)}, u32[]{:S(2)}) collective-permute-start(bf16[2,384,384]{2,1,0:T(8,128)(2,1)S(1)} %get-tuple-element.181), channel_id=1, source_target_pairs={{0,2},{1,3},{2,0},{3,1},{4,6},{5,7},{6,4},{7,5},{8,10},{9,11},{10,... | collective-permute-start | bytes 1769480 | tf_op jit(solution)/shard_map/ppermute | solution.py:663
  151.3 11.2 %collective-permute-start.35 = (bf16[384,384]{1,0:T(8,128)(2,1)S(1)}, bf16[384,384]{1,0:T(8,128)(2,1)S(1)}, u32[]{:S(2)}, u32[]{:S(2)}) collective-permute-start(bf16[384,384]{1,0:T(8,128)(2,1)S(1)} %get-tuple-element.193), channel_id=1, source_target_pairs={{0,2},{1,3},{2,0},{3,1},{4,6},{5,7},{6,4},{7,5},{8,10},{9,11},{10,... | collective-permute-start | bytes 884744 | tf_op jit(solution)/shard_map/ppermute | solution.py:663
  164.9 18.7 %collective-permute-start.38 = (bf16[2,480,384]{2,1,0:T(8,128)(2,1)S(1)}, bf16[2,480,384]{2,1,0:T(8,128)(2,1)S(1)}, u32[]{:S(2)}, u32[]{:S(2)}) collective-permute-start(bf16[2,480,384]{2,1,0:T(8,128)(2,1)S(1)} %get-tuple-element.211), channel_id=1, source_target_pairs={{0,4},{4,0},{1,5},{5,1},{2,6},{6,2},{3,7},{7,3},{8,12},{12,8},{9,1... | collective-permute-start | bytes 2211848 | tf_op jit(solution)/shard_map/ppermute | solution.py:660
  165.5 18.3 %collective-permute-start.39 = (bf16[2,480,384]{2,1,0:T(8,128)(2,1)S(1)}, bf16[2,480,384]{2,1,0:T(8,128)(2,1)S(1)}, u32[]{:S(2)}, u32[]{:S(2)}) collective-permute-start(bf16[2,480,384]{2,1,0:T(8,128)(2,1)S(1)} %get-tuple-element.212), channel_id=1, source_target_pairs={{0,2},{1,3},{2,0},{3,1},{4,6},{5,7},{6,4},{7,5},{8,10},{9,11},{10,... | collective-permute-start | bytes 2211848 | tf_op jit(solution)/shard_map/ppermute | solution.py:663
  172.7 20.1 %collective-permute-start.40 = (bf16[384,384]{1,0:T(8,128)(2,1)S(1)}, bf16[384,384]{1,0:T(8,128)(2,1)S(1)}, u32[]{:S(2)}, u32[]{:S(2)}) collective-permute-start(bf16[384,384]{1,0:T(8,128)(2,1)S(1)} %select_add_fusion.1), channel_id=1, source_target_pairs={{0,16},{8,24},{16,0},{24,8},{1,17},{9,25},{17,1},{25,9},{2,18},{10... | collective-permute-start | bytes 884744 | tf_op jit(solution)/shard_map/ppermute | solution.py:669
  195.3 12.4 %collective-permute-start.45 = (bf16[384,384]{1,0:T(8,128)(2,1)S(1)}, bf16[384,384]{1,0:T(8,128)(2,1)S(1)}, u32[]{:S(2)}, u32[]{:S(2)}) collective-permute-start(bf16[384,384]{1,0:T(8,128)(2,1)S(1)} %add.124), channel_id=1, source_target_pairs={{0,8},{8,0},{16,24},{24,16},{1,9},{9,1},{17,25},{25,17},{2,10},{10... | collective-permute-start | bytes 884744 | tf_op jit(solution)/shard_map/ppermute | solution.py:669
  196.4 16.3 %collective-permute-start.44 = (bf16[480,384]{1,0:T(8,128)(2,1)S(1)}, bf16[480,384]{1,0:T(8,128)(2,1)S(1)}, u32[]{:S(2)}, u32[]{:S(2)}) collective-permute-start(bf16[480,384]{1,0:T(8,128)(2,1)S(1)} %broadcast_select_fusion.2), channel_id=1, source_target_pairs={{0,8},{8,0},{16,24},{24,16},{1,9},{9,1},{17,25},{25,17},{2,10},{10... | collective-permute-start | bytes 1105928 | tf_op jit(solution)/shard_map/ppermute | solution.py:669
  199.2 13.6 %collective-permute-start.46 = (bf16[2,304,384]{2,1,0:T(8,128)(2,1)S(1)}, bf16[2,304,384]{2,1,0:T(8,128)(2,1)S(1)}, u32[]{:S(2)}, u32[]{:S(2)}) collective-permute-start(bf16[2,304,384]{2,1,0:T(8,128)(2,1)S(1)} %fusion.4), channel_id=1, source_target_pairs={{0,4},{4,0},{1,5},{5,1},{2,6},{6,2},{3,7},{7,3},{8,12},{12,8},{9,1... | collective-permute-start | bytes 1400840 | tf_op jit(solution)/shard_map/ppermute | solution.py:660
  200.2 12.6 %collective-permute-start.47 = (bf16[2,304,384]{2,1,0:T(8,128)(2,1)S(1)}, bf16[2,304,384]{2,1,0:T(8,128)(2,1)S(1)}, u32[]{:S(2)}, u32[]{:S(2)}) collective-permute-start(bf16[2,304,384]{2,1,0:T(8,128)(2,1)S(1)} %fusion.3), channel_id=1, source_target_pairs={{0,2},{1,3},{2,0},{3,1},{4,6},{5,7},{6,4},{7,5},{8,10},{9,11},{10,... | collective-permute-start | bytes 1400840 | tf_op jit(solution)/shard_map/ppermute | solution.py:663
  214.9 18.6 %collective-permute-start.51 = (bf16[480,384]{1,0:T(8,128)(2,1)S(1)}, bf16[480,384]{1,0:T(8,128)(2,1)S(1)}, u32[]{:S(2)}, u32[]{:S(2)}) collective-permute-start(bf16[480,384]{1,0:T(8,128)(2,1)S(1)} %select_add_fusion), channel_id=1, source_target_pairs={{0,16},{8,24},{16,0},{24,8},{1,17},{9,25},{17,1},{25,9},{2,18},{10... | collective-permute-start | bytes 1105928 | tf_op jit(solution)/shard_map/ppermute | solution.py:669
  221.6 14.8 %collective-permute-start.50 = (bf16[304,384]{1,0:T(8,128)(2,1)}, bf16[304,384]{1,0:T(8,128)(2,1)}, u32[]{:S(2)}, u32[]{:S(2)}) collective-permute-start(bf16[304,384]{1,0:T(8,128)(2,1)} %broadcast_select_fusion.8), channel_id=1, source_target_pairs={{0,8},{8,0},{16,24},{24,16},{1,9},{9,1},{17,25},{25,17},{2,10},{10... | collective-permute-start | bytes 700424 | tf_op jit(solution)/shard_map/ppermute | solution.py:669
  222.4 39.3 %all-to-all-start.2 = ((bf16[16,96,256]{2,1,0:T(8,128)(2,1)}), bf16[16,96,256]{2,1,0:T(8,128)(2,1)S(1)}, u32[]{:S(2)}, u32[]{:S(2)}) async-start(bf16[16,96,256]{2,1,0:T(8,128)(2,1)} %bitcast.40), calls=%async_computation.2 | async-start | bytes 1572864 | tf_op jit(solution)/shard_map/all_to_all | solution.py:672
  238.6 19.0 %collective-permute-start.54 = (bf16[480,384]{1,0:T(8,128)(2,1)S(1)}, bf16[480,384]{1,0:T(8,128)(2,1)S(1)}, u32[]{:S(2)}, u32[]{:S(2)}) collective-permute-start(bf16[480,384]{1,0:T(8,128)(2,1)S(1)} %add.134), channel_id=1, source_target_pairs={{0,8},{8,0},{16,24},{24,16},{1,9},{9,1},{17,25},{25,17},{2,10},{10... | collective-permute-start | bytes 1105928 | tf_op jit(solution)/shard_map/ppermute | solution.py:669
  247.5 13.7 %collective-permute-start.53 = (bf16[304,384]{1,0:T(8,128)(2,1)S(1)}, bf16[304,384]{1,0:T(8,128)(2,1)S(1)}, u32[]{:S(2)}, u32[]{:S(2)}) collective-permute-start(bf16[304,384]{1,0:T(8,128)(2,1)S(1)} %add.133), channel_id=1, source_target_pairs={{0,8},{8,0},{16,24},{24,16},{1,9},{9,1},{17,25},{25,17},{2,10},{10... | collective-permute-start | bytes 700424 | tf_op jit(solution)/shard_map/ppermute | solution.py:669
  261.7 17.0 %all-to-all-start.1 = ((bf16[16,96,256]{2,1,0:T(8,128)(2,1)}), bf16[16,96,256]{2,1,0:T(8,128)(2,1)S(1)}, u32[]{:S(2)}, u32[]{:S(2)}) async-start(bf16[16,96,256]{2,1,0:T(8,128)(2,1)} %bitcast.38), calls=%async_computation.1 | async-start | bytes 1572864 | tf_op jit(solution)/shard_map/all_to_all | solution.py:672
  (90 other events, 668.8 us)

commit v2 on v1

--- a/solution.py
+++ b/solution.py
@@ -17,6 +17,7 @@
 HBM = pl.BlockSpec(memory_space=pltpu.HBM)
 SMEM = pl.BlockSpec(memory_space=pltpu.SMEM)
 VMEM = pl.BlockSpec(memory_space=pltpu.VMEM)
+LOOSE = pl.BlockSpec(memory_space=pltpu.VMEM)
 root_half = math.sqrt(0.5)
 root_tau = 1.0 / math.sqrt(2.0 * math.pi)
 score_scale = 1.0 / math.sqrt(HEAD)
@@ -134,10 +135,10 @@
     held = [v for v in scratch if v.memory_space == pltpu.VMEM]
     limit = sum(vmem_bytes(v.shape, v.dtype) for v in held) + (ROOM << 20)
     single = not isinstance(outs, tuple)
-    places = [pinned(spec)(v.shape, v.dtype) for v, spec in zip((outs,) if single else outs, (out_specs,) if single else out_specs)]
+    places = [v if spec is LOOSE else pinned(spec)(v.shape, v.dtype) for v, spec in zip((outs,) if single else outs, (out_specs,) if single else out_specs)]
 
     def run(*args):
-        args = [v if spec is SMEM else pltpu.with_memory_space_constraint(v, pinned(spec)) for v, spec in zip(args, in_specs)]
+        args = [v if spec is SMEM or spec is LOOSE else pltpu.with_memory_space_constraint(v, pinned(spec)) for v, spec in zip(args, in_specs)]
         return pl.pallas_call(
             kernel,
             out_shape=places[0] if single else tuple(places),
@@ -824,7 +825,7 @@
     def reduce_far(v, got, name):
         one = sds(v[0].shape[1:], bf16)
         p0, p1, q0, q1 = call(
-            sum_near_kernel, (one, one, one, one), [VMEM] * 4, [VMEM] * 4, **time_us(2), name=name
+            sum_near_kernel, (one, one, one, one), [LOOSE] * 4, [LOOSE] * 4, **time_us(2), name=name
         )(v[0], got[0], v[2], got[1])
         return (p0, q0), (flip_chip(p1), flip_row(q1))
 
@@ -837,7 +838,7 @@
         functools.partial(hidden_back_kernel, nc, rw, fw),
         (sds(hid, bf16), sds((nc, fw, 8), f32)) + (sds(sum3, bf16),) * 4,
         [SMEM] + [VMEM] * 5 + [HBM] * 12,
-        [VMEM] * 6,
+        [VMEM] * 2 + [LOOSE] * 4,
         [vm(hid), vm(hid), vm((nc, fw, nr * rw)), vm(hid, f32), dma((n,)), dma((nc,)), dma((nc,))],
         **time_us(13), name="hidden_back",
     )(info, st, e2, pf, shr_keep, shr_got, vh, slope, *g3)

time: 281 us -> 281 us (level)
  no operation moved by 1% of the time
where the time goes in v2:
time: 281 us; the launch traced here: 280 us
  Pallas kernels  89.5 us (32%)
  waiting for transfers between devices  81.8 us (29%)
  starting transfers between devices  64.9 us (23%)
  local copies, waits for them, and re-layouts  29 us (10%)
  other arithmetic  10.8 us (4%)
  between operations  3.68 us (1%)
    pallas_call x13, Pallas kernels, run(): pl.pallas_call(kernel, out_shape=places[0] if single else tuple(places),...  89.5 us
    ppermute x9, waiting for transfers between devices, flip_dp(): return lax.ppermute(v, 'dp', [(i, i ^ step) for i in range(holders)])  35.9 us
    ppermute x13, waiting for transfers between devices, flip_chip(): return lax.ppermute(v, 'col', [(i, i ^ 2) for i in range(nc)])  29 us
    ppermute x14, starting transfers between devices, flip_row(): return lax.ppermute(v, 'row', [(i, i ^ 1) for i in range(nr)])  20.2 us
    ppermute x13, starting transfers between devices, flip_chip(): return lax.ppermute(v, 'col', [(i, i ^ 2) for i in range(nc)])  14.8 us
    ppermute x9, starting transfers between devices, flip_dp(): return lax.ppermute(v, 'dp', [(i, i ^ step) for i in range(holders)])  14.4 us
    unnamed x129, local copies, waits for them, and re-layouts  12.1 us
    all_to_all x3, starting transfers between devices, exchange(): lax.all_to_all(v, ('dp',) + RC, 0, 0, axis_index_groups=groups, tiled=True)  11.3 us
  transfers between devices with their start and end apart: 58, of which 29 were waited for; matrix products, arithmetic and copies ran while one was open for 9% of the time, Pallas kernels for 28%

profile of v2, /device:TPU:0, one launch (start us, length us, event | category | flops | bytes accessed | tf_op | source)
XLA Modules:
  0.0 279.6 jit_solution(16580264374652621827)
XLA Ops:
  1.9 3.0 %collective-permute-start.1 = (bf16[768,384]{1,0:T(8,128)(2,1)S(1)}, bf16[768,384]{1,0:T(8,128)(2,1)}, u32[]{:S(2)}, u32[]{:S(2)}) collective-permute-start(bf16[768,384]{1,0:T(8,128)(2,1)S(1)} %pad_maximum_fusion.2.refs_0_), channel_id=1, source_target_pairs={{0,2},{1,3},{2,0},{3,1},{4,6},{5,7},{6,4},{7,5},{8,10},{9,11},{10,... | collective-permute-start | bytes 1769480 | tf_op jit(solution)/shard_map/ppermute | solution.py:664
  15.2 3.1 %collective-permute-done.1.refs_2_ = bf16[768,384]{1,0:T(8,128)(2,1)} collective-permute-done((bf16[768,384]{1,0:T(8,128)(2,1)S(1)}, bf16[768,384]{1,0:T(8,128)(2,1)}, u32[]{:S(2)}, u32[]{:S(2)}) %collective-permute-start.1) | collective-permute-done | bytes 589856 | tf_op jit(solution)/shard_map/ppermute | solution.py:664
  19.8 3.9 %all-to-all-start = ((bf16[16,192,256]{2,1,0:T(8,128)(2,1)}), bf16[16,192,256]{2,1,0:T(8,128)(2,1)S(1)}, u32[]{:S(2)}, u32[]{:S(2)}) async-start(bf16[16,192,256]{2,1,0:T(8,128)(2,1)} %bitcast.18), calls=%async_computation | async-start | bytes 3145728 | tf_op jit(solution)/shard_map/all_to_all | solution.py:673
  27.9 14.8 %collective-permute-done.7 = f32[96,128]{1,0:T(8,128)S(1)} collective-permute-done((f32[96,128]{1,0:T(8,128)S(1)}, f32[96,128]{1,0:T(8,128)S(1)}, u32[]{:S(2)}, u32[]{:S(2)}) %collective-permute-start.7) | collective-permute-done | bytes 49184 | tf_op jit(solution)/shard_map/ppermute | solution.py:664
  42.7 3.6 %collective-permute-start.9 = (f32[96,128]{1,0:T(8,128)S(1)}, f32[96,128]{1,0:T(8,128)S(1)}, u32[]{:S(2)}, u32[]{:S(2)}) collective-permute-start(f32[96,128]{1,0:T(8,128)S(1)} %collective-permute-done.7), channel_id=1, source_target_pairs={{0,4},{4,0},{1,5},{5,1},{2,6},{6,2},{3,7},{7,3},{8,12},{12,8},{9,1... | collective-permute-start | bytes 147464 | tf_op jit(solution)/shard_map/ppermute | solution.py:661
  59.9 11.9 %attend.1 = (bf16[768,512]{1,0:T(8,128)(2,1)S(1)}, bf16[768,512]{1,0:T(8,128)(2,1)S(1)}, bf16[4,576,512]{2,1,0:T(8,128)(2,1)}, f32[4,8,512]{2,1,0:T(8,128)S(1)},...) custom-call(s32[5]{0:T(128)S(1)} %pad_add_fusion.info, ...), custom_call_target="tpu_custom_call" | custom-call | flops 12999999488 | bytes 13000000 | tf_op jit(solution)/shard_map/attend/pallas_call | solution.py:142
  76.7 3.8 %output.1 = (bf16[768,512]{1,0:T(8,128)(2,1)S(1)}, f32[768,512]{1,0:T(8,128)S(1)}, bf16[768,512]{1,0:T(8,128)(2,1)S(1)}) custom-call(s32[5]{0:T(128)S(1)} %pad_add_fusion.info, bf16[768,512]{1,0:T(8,128)(2,1)S(1)} %get-tuple-element.146.x_ref, f32[768,512]{1,0:T(8,128)S(1)} %get-tuple-element.145.o_ref, f32[768,16]{1,0:T(8,128)S(1)} %get-tuple-element.147.pd, ...), custom_call_target="tpu_custom_call" | custom-call | flops 5000000000 | bytes 5000000 | tf_op jit(solution)/shard_map/output/pallas_call | solution.py:142
  80.5 2.5 collective-permute-done.16.refs_7_
  87.2 11.6 %expand.1 = (bf16[4,768,512]{2,1,0:T(8,128)(2,1)S(1)}, bf16[4,768,512]{2,1,0:T(8,128)(2,1)}, bf16[4,768,512]{2,1,0:T(8,128)(2,1)}, f32[8,512]{1,0:T(8,128)S(1)}) custom-call(s32[5]{0:T(128)S(1)} %pad_add_fusion.info, bf16[768,512]{1,0:T(8,128)(2,1)S(1)} %get-tuple-element.151.b_ref, f32[4,768,8]{2,1,0:T(8,128)S(1)} %get-tuple-element.152.pf, ...), custom_call_target="tpu_custom_call" | custom-call | flops 12999999488 | bytes 13000000 | tf_op jit(solution)/shard_map/expand/pallas_call | solution.py:142
  104.1 3.5 %shrink_grads.1 = (bf16[768,512]{1,0:T(8,128)(2,1)S(1)}, bf16[2,2,768,384]{3,2,1,0:T(8,128)(2,1)S(1)}, bf16[2,2,768,384]{3,2,1,0:T(8,128)(2,1)S(1)}) custom-call(s32[5]{0:T(128)S(1)} %pad_add_fusion.info, bf16[4,768,512]{2,1,0:T(8,128)(2,1)S(1)} %get-tuple-element.228.gn_ref, bf16[2,8,192,256]{3,2,1,0:T(8,128)(2,1)S(1)} %bitcast.111), custom_call_target="tpu_custom_call" | custom-call | flops 7000000000 | bytes 7000000 | tf_op jit(solution)/shard_map/shrink_grads/pallas_call | solution.py:142
  107.7 2.9 %collective-permute-done.25.refs_7_ = bf16[384,384]{1,0:T(8,128)(2,1)S(1)} collective-permute-done((bf16[384,384]{1,0:T(8,128)(2,1)S(1)}, bf16[384,384]{1,0:T(8,128)(2,1)S(1)}, u32[]{:S(2)}, u32[]{:S(2)}) %collective-permute-start.25) | collective-permute-done | bytes 294944 | tf_op jit(solution)/shard_map/ppermute | solution.py:664
  111.8 4.4 %collective-permute-done.30.refs_8_ = bf16[384,384]{1,0:T(8,128)(2,1)S(1)} collective-permute-done((bf16[384,384]{1,0:T(8,128)(2,1)S(1)}, bf16[384,384]{1,0:T(8,128)(2,1)S(1)}, u32[]{:S(2)}, u32[]{:S(2)}) %collective-permute-start.30) | collective-permute-done | bytes 294944 | tf_op jit(solution)/shard_map/ppermute | solution.py:667
  117.3 10.3 %hidden_back.1 = (bf16[4,768,512]{2,1,0:T(8,128)(2,1)S(1)}, f32[4,768,8]{2,1,0:T(8,128)S(1)}, bf16[2,384,384]{2,1,0:T(8,128)(2,1)S(1)}, bf16[2,384,384]{2,1,0:T(...) custom-call(s32[5]{0:T(128)S(1)} %pad_add_fusion.info, ...), custom_call_target="tpu_custom_call" | custom-call | flops 12999999488 | bytes 13000000 | tf_op jit(solution)/shard_map/hidden_back/pallas_call | solution.py:142
  129.8 7.5 %middle_back.1 = (f32[768,512]{1,0:T(8,128)S(1)}, bf16[768,512]{1,0:T(8,128)(2,1)S(1)}, f32[768,8]{1,0:T(8,128)S(1)}) custom-call(s32[5]{0:T(128)S(1)} %pad_add_fusion.info, bf16[4,768,512]{2,1,0:T(8,128)(2,1)S(1)} %get-tuple-element.175.df_ref, f32[768,512]{1,0:T(8,128)S(1)} %get-tuple-element.176.x1_ref, bf16[768,512]{1,0:T(8,128)(2,1)S(1)} %get-tuple-element.162.e2_ref, ...), custom_call_target="tpu_custom_call" | custom-call | flops 8000000000 | bytes 8000000 | tf_op jit(solution)/shard_map/middle_back/pallas_call | solution.py:142
  139.3 6.0 %middle_grads.1 = (bf16[2,2,960,384]{3,2,1,0:T(8,128)(2,1)S(1)}, bf16[2,2,960,384]{3,2,1,0:T(8,128)(2,1)}) custom-call(s32[5]{0:T(128)S(1)} %pad_add_fusion.info, bf16[768,512]{1,0:T(8,128)(2,1)S(1)} %get-tuple-element.151.b_ref, bf16[4,768,512]{2,1,0:T(8,128)(2,1)S(1)} %get-tuple-element.175.df_ref, bf16[4,192,512]{2,1,0:T(8,128)(2,1)S(1)} %bitcast.113, ...), custom_call_target="tpu_custom_call" | custom-call | flops 7000000000 | bytes 7000000 | tf_op jit(solution)/shard_map/middle_grads/pallas_call | solution.py:142
  153.6 8.9 %attend_back.1 = (bf16[2304,512]{1,0:T(8,128)(2,1)S(1)}, f32[768,8]{1,0:T(8,128)S(1)}, f32[4,192,8]{2,1,0:T(8,128)S(1)}, bf16[768,512]{1,0:T(8,128)(2,1)S(1)}, b...) custom-call(s32[5]{0:T(128)S(1)} %pad_add_fusion.info, ...), custom_call_target="tpu_custom_call" | custom-call | flops 11000000512 | bytes 11000000 | tf_op jit(solution)/shard_map/attend_back/pallas_call | solution.py:142
  166.8 4.8 %attend_back_rest.1 = (bf16[2304,512]{1,0:T(8,128)(2,1)S(1)}, f32[4,192,8]{2,1,0:T(8,128)S(1)}) custom-call(s32[5]{0:T(128)S(1)} %pad_add_fusion.info, f32[768,512]{1,0:T(8,128)S(1)} %copy-done.13, bf16[4,576,512]{2,1,0:T(8,128)(2,1)S(1)} %get-tuple-element.187.qkv_ref, f32[4,8,512]{2,1,0:T(8,128)S(1)} %copy-done.31, ...), custom_call_target="tpu_custom_call", output_to_operand_aliasing={{0}: (5, {}), {1}: (6, {})} | custom-call | flops 8000000000 | bytes 8000000 | tf_op jit(solution)/shard_map/attend_back_rest/pallas_call | solution.py:142
  172.7 2.6 collective-permute-start.40
  175.4 8.3 %input_back.1 = (bf16[2,768,256]{2,1,0:T(8,128)(2,1)}, f32[768,8]{1,0:T(8,128)S(1)}) custom-call(s32[5]{0:T(128)S(1)} %pad_add_fusion.info, bf16[2304,512]{1,0:T(8,128)(2,1)S(1)} %get-tuple-element.207.dqkv, bf16[768,512]{1,0:T(8,128)(2,1)S(1)} %copy-done.17, f32[768,512]{1,0:T(8,128)S(1)} %copy-done.19, f32[768,16]{1,0:T(8,128)S(1)} %copy-done.23, ...), custom_call_target="tpu_custom_call" | custom-call | flops 7000000000 | bytes 7000000 | tf_op jit(solution)/shard_map/input_back/pallas_call | solution.py:142
  186.6 6.2 %attend_grads.1 = (bf16[2,2,608,384]{3,2,1,0:T(8,128)(2,1)S(1)}, bf16[2,2,608,384]{3,2,1,0:T(8,128)(2,1)S(1)}) custom-call(s32[5]{0:T(128)S(1)} %pad_add_fusion.info, bf16[2304,512]{1,0:T(8,128)(2,1)S(1)} %get-tuple-element.207.dqkv, bf16[768,512]{1,0:T(8,128)(2,1)S(1)} %copy-done.27, f32[768,8]{1,0:T(8,128)S(1)} %get-tuple-element.213.gd_in, ...), custom_call_target="tpu_custom_call" | custom-call | flops 7000000000 | bytes 7000000 | tf_op jit(solution)/shard_map/attend_grads/pallas_call | solution.py:142
  201.1 6.6 %shrink.1 = bf16[2,768,256]{2,1,0:T(8,128)(2,1)} custom-call(s32[5]{0:T(128)S(1)} %pad_add_fusion.info, f32[768,16]{1,0:T(8,128)S(1)} %copy-done.23, bf16[3072,512]{1,0:T(8,128)(2,1)S(1)} %bitcast.112, f32[768,512]{1,0:T(8,128)S(1)} %copy-done.11, bf16[768,384]{1,0:T(8,128)(2,1)} %refs_0_.3, bf16[768,384]{1,0:T(8,128)(2,1)} %copy-done.47, ...), custom_call_target="tpu_custom_call" | custom-call | flops 8000000000 | bytes 8000000 | tf_op jit(solution)/shard_map/shrink/pallas_call | solution.py:142
  207.7 5.0 %collective-permute-done.44 = bf16[480,384]{1,0:T(8,128)(2,1)S(1)} collective-permute-done((bf16[480,384]{1,0:T(8,128)(2,1)S(1)}, bf16[480,384]{1,0:T(8,128)(2,1)S(1)}, u32[]{:S(2)}, u32[]{:S(2)}) %collective-permute-start.44) | collective-permute-done | bytes 368672 | tf_op jit(solution)/shard_map/ppermute | solution.py:670
  217.3 3.1 %collective-permute-done.48 = bf16[304,384]{1,0:T(8,128)(2,1)S(1)} collective-permute-done((bf16[304,384]{1,0:T(8,128)(2,1)S(1)}, bf16[304,384]{1,0:T(8,128)(2,1)S(1)}, u32[]{:S(2)}, u32[]{:S(2)}) %collective-permute-start.48) | collective-permute-done | bytes 233504 | tf_op jit(solution)/shard_map/ppermute | solution.py:664
  222.4 3.8 %all-to-all-start.2 = ((bf16[16,96,256]{2,1,0:T(8,128)(2,1)}), bf16[16,96,256]{2,1,0:T(8,128)(2,1)S(1)}, u32[]{:S(2)}, u32[]{:S(2)}) async-start(bf16[16,96,256]{2,1,0:T(8,128)(2,1)} %bitcast.40), calls=%async_computation.2 | async-start | bytes 1572864 | tf_op jit(solution)/shard_map/all_to_all | solution.py:673
  226.2 7.2 %collective-permute-done.51 = bf16[480,384]{1,0:T(8,128)(2,1)S(1)} collective-permute-done((bf16[480,384]{1,0:T(8,128)(2,1)S(1)}, bf16[480,384]{1,0:T(8,128)(2,1)S(1)}, u32[]{:S(2)}, u32[]{:S(2)}) %collective-permute-start.51) | collective-permute-done | bytes 368672 | tf_op jit(solution)/shard_map/ppermute | solution.py:670
  233.4 2.9 %collective-permute-done.50 = bf16[304,384]{1,0:T(8,128)(2,1)} collective-permute-done((bf16[304,384]{1,0:T(8,128)(2,1)}, bf16[304,384]{1,0:T(8,128)(2,1)}, u32[]{:S(2)}, u32[]{:S(2)}) %collective-permute-start.50) | collective-permute-done | bytes 233504 | tf_op jit(solution)/shard_map/ppermute | solution.py:670
  238.6 2.5 collective-permute-start.54
  241.2 6.2 %collective-permute-done.52 = bf16[304,384]{1,0:T(8,128)(2,1)S(1)} collective-permute-done((bf16[304,384]{1,0:T(8,128)(2,1)S(1)}, bf16[304,384]{1,0:T(8,128)(2,1)S(1)}, u32[]{:S(2)}, u32[]{:S(2)}) %collective-permute-start.52) | collective-permute-done | bytes 233504 | tf_op jit(solution)/shard_map/ppermute | solution.py:670
  247.8 9.9 %collective-permute-done.54 = bf16[480,384]{1,0:T(8,128)(2,1)S(1)} collective-permute-done((bf16[480,384]{1,0:T(8,128)(2,1)S(1)}, bf16[480,384]{1,0:T(8,128)(2,1)S(1)}, u32[]{:S(2)}, u32[]{:S(2)}) %collective-permute-start.54) | collective-permute-done | bytes 368672 | tf_op jit(solution)/shard_map/ppermute | solution.py:670
  257.6 3.6 %collective-permute-done.53 = bf16[304,384]{1,0:T(8,128)(2,1)S(1)} collective-permute-done((bf16[304,384]{1,0:T(8,128)(2,1)S(1)}, bf16[304,384]{1,0:T(8,128)(2,1)S(1)}, u32[]{:S(2)}, u32[]{:S(2)}) %collective-permute-start.53) | collective-permute-done | bytes 233504 | tf_op jit(solution)/shard_map/ppermute | solution.py:670
  261.7 3.6 %all-to-all-start.1 = ((bf16[16,96,256]{2,1,0:T(8,128)(2,1)}), bf16[16,96,256]{2,1,0:T(8,128)(2,1)S(1)}, u32[]{:S(2)}, u32[]{:S(2)}) async-start(bf16[16,96,256]{2,1,0:T(8,128)(2,1)} %bitcast.38), calls=%async_computation.1 | async-start | bytes 1572864 | tf_op jit(solution)/shard_map/all_to_all | solution.py:673
  275.3 3.4 %all-to-all-done.1 = bf16[16,96,256]{2,1,0:T(8,128)(2,1)S(1)} async-done(((bf16[16,96,256]{2,1,0:T(8,128)(2,1)}), bf16[16,96,256]{2,1,0:T(8,128)(2,1)S(1)}, u32[]{:S(2)}, u32[]{:S(2)}) %all-to-all-start.1) | async-done | bytes 786464 | tf_op jit(solution)/shard_map/all_to_all | solution.py:673
  (302 shorter events, 94.5 us)
Async XLA Ops:
  1.9 16.5 %collective-permute-start.1 = (bf16[768,384]{1,0:T(8,128)(2,1)S(1)}, bf16[768,384]{1,0:T(8,128)(2,1)}, u32[]{:S(2)}, u32[]{:S(2)}) collective-permute-start(bf16[768,384]{1,0:T(8,128)(2,1)S(1)} %pad_maximum_fusion.2.refs_0_), channel_id=1, source_target_pairs={{0,2},{1,3},{2,0},{3,1},{4,6},{5,7},{6,4},{7,5},{8,10},{9,11},{10,... | collective-permute-start | bytes 1769480 | tf_op jit(solution)/shard_map/ppermute | solution.py:664
  5.0 14.9 %collective-permute-start = (bf16[768,384]{1,0:T(8,128)(2,1)S(1)}, bf16[768,384]{1,0:T(8,128)(2,1)}, u32[]{:S(2)}, u32[]{:S(2)}) collective-permute-start(bf16[768,384]{1,0:T(8,128)(2,1)S(1)} %pad_maximum_fusion.2.refs_0_), channel_id=1, source_target_pairs={{0,4},{4,0},{1,5},{5,1},{2,6},{6,2},{3,7},{7,3},{8,12},{12,8},{9,1... | collective-permute-start | bytes 1769480 | tf_op jit(solution)/shard_map/ppermute | solution.py:661
  19.8 35.8 %all-to-all-start = ((bf16[16,192,256]{2,1,0:T(8,128)(2,1)}), bf16[16,192,256]{2,1,0:T(8,128)(2,1)S(1)}, u32[]{:S(2)}, u32[]{:S(2)}) async-start(bf16[16,192,256]{2,1,0:T(8,128)(2,1)} %bitcast.18), calls=%async_computation | async-start | bytes 3145728 | tf_op jit(solution)/shard_map/all_to_all | solution.py:673
  23.7 27.1 %collective-permute-start.4 = (bf16[768,384]{1,0:T(8,128)(2,1)S(1)}, bf16[768,384]{1,0:T(8,128)(2,1)S(1)}, u32[]{:S(2)}, u32[]{:S(2)}) collective-permute-start(bf16[768,384]{1,0:T(8,128)(2,1)S(1)} %pad_maximum_fusion.2.refs_0_), channel_id=1, source_target_pairs={{0,1},{1,0},{2,3},{3,2},{4,5},{5,4},{6,7},{7,6},{8,9},{9,8},{10,11... | collective-permute-start | bytes 1769480 | tf_op jit(solution)/shard_map/ppermute | solution.py:667
  24.2 31.4 %collective-permute-start.5 = (bf16[768,384]{1,0:T(8,128)(2,1)}, bf16[768,384]{1,0:T(8,128)(2,1)}, u32[]{:S(2)}, u32[]{:S(2)}) collective-permute-start(bf16[768,384]{1,0:T(8,128)(2,1)} %collective-permute-done.1.refs_2_), channel_id=1, source_target_pairs={{0,1},{1,0},{2,3},{3,2},{4,5},{5,4},{6,7},{7,6},{8,9},{9,8},{10,11... | collective-permute-start | bytes 1769480 | tf_op jit(solution)/shard_map/ppermute | solution.py:667
  24.3 31.3 %collective-permute-start.6 = (bf16[768,384]{1,0:T(8,128)(2,1)}, bf16[768,384]{1,0:T(8,128)(2,1)}, u32[]{:S(2)}, u32[]{:S(2)}) collective-permute-start(bf16[768,384]{1,0:T(8,128)(2,1)} %collective-permute-done.refs_4_), channel_id=1, source_target_pairs={{0,1},{1,0},{2,3},{3,2},{4,5},{5,4},{6,7},{7,6},{8,9},{9,8},{10,11... | collective-permute-start | bytes 1769480 | tf_op jit(solution)/shard_map/ppermute | solution.py:667
  24.7 17.9 %collective-permute-start.7 = (f32[96,128]{1,0:T(8,128)S(1)}, f32[96,128]{1,0:T(8,128)S(1)}, u32[]{:S(2)}, u32[]{:S(2)}) collective-permute-start(f32[96,128]{1,0:T(8,128)S(1)} %pad_bitcast_fusion), channel_id=1, source_target_pairs={{0,2},{1,3},{2,0},{3,1},{4,6},{5,7},{6,4},{7,5},{8,10},{9,11},{10,... | collective-permute-start | bytes 147464 | tf_op jit(solution)/shard_map/ppermute | solution.py:664
  26.4 21.8 %collective-permute-start.8 = (f32[96,128]{1,0:T(8,128)S(1)}, f32[96,128]{1,0:T(8,128)S(1)}, u32[]{:S(2)}, u32[]{:S(2)}) collective-permute-start(f32[96,128]{1,0:T(8,128)S(1)} %pad_bitcast_fusion), channel_id=1, source_target_pairs={{0,4},{4,0},{1,5},{5,1},{2,6},{6,2},{3,7},{7,3},{8,12},{12,8},{9,1... | collective-permute-start | bytes 147464 | tf_op jit(solution)/shard_map/ppermute | solution.py:661
  56.3 24.2 %collective-permute-start.17 = (bf16[384,768]{1,0:T(8,128)(2,1)}, bf16[384,768]{1,0:T(8,128)(2,1)S(1)}, u32[]{:S(2)}, u32[]{:S(2)}) collective-permute-start(bf16[384,768]{1,0:T(8,128)(2,1)} %refs_0_.2), channel_id=1, source_target_pairs={{0,1},{1,0},{2,3},{3,2},{4,5},{5,4},{6,7},{7,6},{8,9},{9,8},{10,11... | collective-permute-start | bytes 1769480 | tf_op jit(solution)/shard_map/ppermute | solution.py:667
  56.5 15.8 %collective-permute-start.14 = (bf16[384,768]{1,0:T(8,128)(2,1)}, bf16[384,768]{1,0:T(8,128)(2,1)S(1)}, u32[]{:S(2)}, u32[]{:S(2)}) collective-permute-start(bf16[384,768]{1,0:T(8,128)(2,1)} %refs_0_.2), channel_id=1, source_target_pairs={{0,2},{1,3},{2,0},{3,1},{4,6},{5,7},{6,4},{7,5},{8,10},{9,11},{10,... | collective-permute-start | bytes 1769480 | tf_op jit(solution)/shard_map/ppermute | solution.py:664
  57.9 15.6 %collective-permute-start.13 = (bf16[384,768]{1,0:T(8,128)(2,1)}, bf16[384,768]{1,0:T(8,128)(2,1)S(1)}, u32[]{:S(2)}, u32[]{:S(2)}) collective-permute-start(bf16[384,768]{1,0:T(8,128)(2,1)} %refs_0_.2), channel_id=1, source_target_pairs={{0,4},{4,0},{1,5},{5,1},{2,6},{6,2},{3,7},{7,3},{8,12},{12,8},{9,1... | collective-permute-start | bytes 1769480 | tf_op jit(solution)/shard_map/ppermute | solution.py:661
  84.2 23.5 %collective-permute-start.26 = (bf16[768,384]{1,0:T(8,128)(2,1)S(1)}, bf16[768,384]{1,0:T(8,128)(2,1)S(1)}, u32[]{:S(2)}, u32[]{:S(2)}) collective-permute-start(bf16[768,384]{1,0:T(8,128)(2,1)S(1)} %copy-done.45), channel_id=1, source_target_pairs={{0,1},{1,0},{2,3},{3,2},{4,5},{5,4},{6,7},{7,6},{8,9},{9,8},{10,11... | collective-permute-start | bytes 1769480 | tf_op jit(solution)/shard_map/ppermute | solution.py:667
  84.3 15.7 %collective-permute-start.23 = (bf16[768,384]{1,0:T(8,128)(2,1)S(1)}, bf16[768,384]{1,0:T(8,128)(2,1)S(1)}, u32[]{:S(2)}, u32[]{:S(2)}) collective-permute-start(bf16[768,384]{1,0:T(8,128)(2,1)S(1)} %copy-done.45), channel_id=1, source_target_pairs={{0,2},{1,3},{2,0},{3,1},{4,6},{5,7},{6,4},{7,5},{8,10},{9,11},{10,... | collective-permute-start | bytes 1769480 | tf_op jit(solution)/shard_map/ppermute | solution.py:664
  85.5 15.4 %collective-permute-start.22 = (bf16[768,384]{1,0:T(8,128)(2,1)S(1)}, bf16[768,384]{1,0:T(8,128)(2,1)S(1)}, u32[]{:S(2)}, u32[]{:S(2)}) collective-permute-start(bf16[768,384]{1,0:T(8,128)(2,1)S(1)} %copy-done.45), channel_id=1, source_target_pairs={{0,4},{4,0},{1,5},{5,1},{2,6},{6,2},{3,7},{7,3},{8,12},{12,8},{9,1... | collective-permute-start | bytes 1769480 | tf_op jit(solution)/shard_map/ppermute | solution.py:661
  100.9 10.2 %collective-permute-start.27 = (bf16[768,384]{1,0:T(8,128)(2,1)S(1)}, bf16[768,384]{1,0:T(8,128)(2,1)S(1)}, u32[]{:S(2)}, u32[]{:S(2)}) collective-permute-start(bf16[768,384]{1,0:T(8,128)(2,1)S(1)} %collective-permute-done.23.refs_2_), channel_id=1, source_target_pairs={{0,1},{1,0},{2,3},{3,2},{4,5},{5,4},{6,7},{7,6},{8,9},{9,8},{10,11... | collective-permute-start | bytes 1769480 | tf_op jit(solution)/shard_map/ppermute | solution.py:667
  101.1 10.1 %collective-permute-start.28 = (bf16[768,384]{1,0:T(8,128)(2,1)S(1)}, bf16[768,384]{1,0:T(8,128)(2,1)S(1)}, u32[]{:S(2)}, u32[]{:S(2)}) collective-permute-start(bf16[768,384]{1,0:T(8,128)(2,1)S(1)} %collective-permute-done.22.refs_4_), channel_id=1, source_target_pairs={{0,1},{1,0},{2,3},{3,2},{4,5},{5,4},{6,7},{7,6},{8,9},{9,8},{10,11... | collective-permute-start | bytes 1769480 | tf_op jit(solution)/shard_map/ppermute | solution.py:667
  127.6 19.3 %collective-permute-start.32 = (bf16[2,384,384]{2,1,0:T(8,128)(2,1)S(1)}, bf16[2,384,384]{2,1,0:T(8,128)(2,1)S(1)}, u32[]{:S(2)}, u32[]{:S(2)}) collective-permute-start(bf16[2,384,384]{2,1,0:T(8,128)(2,1)S(1)} %get-tuple-element.180), channel_id=1, source_target_pairs={{0,4},{4,0},{1,5},{5,1},{2,6},{6,2},{3,7},{7,3},{8,12},{12,8},{9,1... | collective-permute-start | bytes 1769480 | tf_op jit(solution)/shard_map/ppermute | solution.py:661
  129.4 17.5 %collective-permute-start.33 = (bf16[2,384,384]{2,1,0:T(8,128)(2,1)S(1)}, bf16[2,384,384]{2,1,0:T(8,128)(2,1)S(1)}, u32[]{:S(2)}, u32[]{:S(2)}) collective-permute-start(bf16[2,384,384]{2,1,0:T(8,128)(2,1)S(1)} %get-tuple-element.181), channel_id=1, source_target_pairs={{0,2},{1,3},{2,0},{3,1},{4,6},{5,7},{6,4},{7,5},{8,10},{9,11},{10,... | collective-permute-start | bytes 1769480 | tf_op jit(solution)/shard_map/ppermute | solution.py:664
  151.3 11.2 %collective-permute-start.35 = (bf16[384,384]{1,0:T(8,128)(2,1)S(1)}, bf16[384,384]{1,0:T(8,128)(2,1)S(1)}, u32[]{:S(2)}, u32[]{:S(2)}) collective-permute-start(bf16[384,384]{1,0:T(8,128)(2,1)S(1)} %get-tuple-element.193), channel_id=1, source_target_pairs={{0,2},{1,3},{2,0},{3,1},{4,6},{5,7},{6,4},{7,5},{8,10},{9,11},{10,... | collective-permute-start | bytes 884744 | tf_op jit(solution)/shard_map/ppermute | solution.py:664
  164.9 18.7 %collective-permute-start.38 = (bf16[2,480,384]{2,1,0:T(8,128)(2,1)S(1)}, bf16[2,480,384]{2,1,0:T(8,128)(2,1)S(1)}, u32[]{:S(2)}, u32[]{:S(2)}) collective-permute-start(bf16[2,480,384]{2,1,0:T(8,128)(2,1)S(1)} %get-tuple-element.211), channel_id=1, source_target_pairs={{0,4},{4,0},{1,5},{5,1},{2,6},{6,2},{3,7},{7,3},{8,12},{12,8},{9,1... | collective-permute-start | bytes 2211848 | tf_op jit(solution)/shard_map/ppermute | solution.py:661
  165.5 18.3 %collective-permute-start.39 = (bf16[2,480,384]{2,1,0:T(8,128)(2,1)S(1)}, bf16[2,480,384]{2,1,0:T(8,128)(2,1)S(1)}, u32[]{:S(2)}, u32[]{:S(2)}) collective-permute-start(bf16[2,480,384]{2,1,0:T(8,128)(2,1)S(1)} %get-tuple-element.212), channel_id=1, source_target_pairs={{0,2},{1,3},{2,0},{3,1},{4,6},{5,7},{6,4},{7,5},{8,10},{9,11},{10,... | collective-permute-start | bytes 2211848 | tf_op jit(solution)/shard_map/ppermute | solution.py:664
  172.7 20.1 %collective-permute-start.40 = (bf16[384,384]{1,0:T(8,128)(2,1)S(1)}, bf16[384,384]{1,0:T(8,128)(2,1)S(1)}, u32[]{:S(2)}, u32[]{:S(2)}) collective-permute-start(bf16[384,384]{1,0:T(8,128)(2,1)S(1)} %select_add_fusion.1), channel_id=1, source_target_pairs={{0,16},{8,24},{16,0},{24,8},{1,17},{9,25},{17,1},{25,9},{2,18},{10... | collective-permute-start | bytes 884744 | tf_op jit(solution)/shard_map/ppermute | solution.py:670
  195.3 12.4 %collective-permute-start.45 = (bf16[384,384]{1,0:T(8,128)(2,1)S(1)}, bf16[384,384]{1,0:T(8,128)(2,1)S(1)}, u32[]{:S(2)}, u32[]{:S(2)}) collective-permute-start(bf16[384,384]{1,0:T(8,128)(2,1)S(1)} %add.124), channel_id=1, source_target_pairs={{0,8},{8,0},{16,24},{24,16},{1,9},{9,1},{17,25},{25,17},{2,10},{10... | collective-permute-start | bytes 884744 | tf_op jit(solution)/shard_map/ppermute | solution.py:670
  196.4 16.3 %collective-permute-start.44 = (bf16[480,384]{1,0:T(8,128)(2,1)S(1)}, bf16[480,384]{1,0:T(8,128)(2,1)S(1)}, u32[]{:S(2)}, u32[]{:S(2)}) collective-permute-start(bf16[480,384]{1,0:T(8,128)(2,1)S(1)} %broadcast_select_fusion.2), channel_id=1, source_target_pairs={{0,8},{8,0},{16,24},{24,16},{1,9},{9,1},{17,25},{25,17},{2,10},{10... | collective-permute-start | bytes 1105928 | tf_op jit(solution)/shard_map/ppermute | solution.py:670
  199.2 13.6 %collective-permute-start.46 = (bf16[2,304,384]{2,1,0:T(8,128)(2,1)S(1)}, bf16[2,304,384]{2,1,0:T(8,128)(2,1)S(1)}, u32[]{:S(2)}, u32[]{:S(2)}) collective-permute-start(bf16[2,304,384]{2,1,0:T(8,128)(2,1)S(1)} %fusion.4), channel_id=1, source_target_pairs={{0,4},{4,0},{1,5},{5,1},{2,6},{6,2},{3,7},{7,3},{8,12},{12,8},{9,1... | collective-permute-start | bytes 1400840 | tf_op jit(solution)/shard_map/ppermute | solution.py:661
  200.2 12.6 %collective-permute-start.47 = (bf16[2,304,384]{2,1,0:T(8,128)(2,1)S(1)}, bf16[2,304,384]{2,1,0:T(8,128)(2,1)S(1)}, u32[]{:S(2)}, u32[]{:S(2)}) collective-permute-start(bf16[2,304,384]{2,1,0:T(8,128)(2,1)S(1)} %fusion.3), channel_id=1, source_target_pairs={{0,2},{1,3},{2,0},{3,1},{4,6},{5,7},{6,4},{7,5},{8,10},{9,11},{10,... | collective-permute-start | bytes 1400840 | tf_op jit(solution)/shard_map/ppermute | solution.py:664
  214.9 18.6 %collective-permute-start.51 = (bf16[480,384]{1,0:T(8,128)(2,1)S(1)}, bf16[480,384]{1,0:T(8,128)(2,1)S(1)}, u32[]{:S(2)}, u32[]{:S(2)}) collective-permute-start(bf16[480,384]{1,0:T(8,128)(2,1)S(1)} %select_add_fusion), channel_id=1, source_target_pairs={{0,16},{8,24},{16,0},{24,8},{1,17},{9,25},{17,1},{25,9},{2,18},{10... | collective-permute-start | bytes 1105928 | tf_op jit(solution)/shard_map/ppermute | solution.py:670
  221.6 14.8 %collective-permute-start.50 = (bf16[304,384]{1,0:T(8,128)(2,1)}, bf16[304,384]{1,0:T(8,128)(2,1)}, u32[]{:S(2)}, u32[]{:S(2)}) collective-permute-start(bf16[304,384]{1,0:T(8,128)(2,1)} %broadcast_select_fusion.8), channel_id=1, source_target_pairs={{0,8},{8,0},{16,24},{24,16},{1,9},{9,1},{17,25},{25,17},{2,10},{10... | collective-permute-start | bytes 700424 | tf_op jit(solution)/shard_map/ppermute | solution.py:670
  222.4 39.3 %all-to-all-start.2 = ((bf16[16,96,256]{2,1,0:T(8,128)(2,1)}), bf16[16,96,256]{2,1,0:T(8,128)(2,1)S(1)}, u32[]{:S(2)}, u32[]{:S(2)}) async-start(bf16[16,96,256]{2,1,0:T(8,128)(2,1)} %bitcast.40), calls=%async_computation.2 | async-start | bytes 1572864 | tf_op jit(solution)/shard_map/all_to_all | solution.py:673
  238.6 19.0 %collective-permute-start.54 = (bf16[480,384]{1,0:T(8,128)(2,1)S(1)}, bf16[480,384]{1,0:T(8,128)(2,1)S(1)}, u32[]{:S(2)}, u32[]{:S(2)}) collective-permute-start(bf16[480,384]{1,0:T(8,128)(2,1)S(1)} %add.134), channel_id=1, source_target_pairs={{0,8},{8,0},{16,24},{24,16},{1,9},{9,1},{17,25},{25,17},{2,10},{10... | collective-permute-start | bytes 1105928 | tf_op jit(solution)/shard_map/ppermute | solution.py:670
  247.5 13.7 %collective-permute-start.53 = (bf16[304,384]{1,0:T(8,128)(2,1)S(1)}, bf16[304,384]{1,0:T(8,128)(2,1)S(1)}, u32[]{:S(2)}, u32[]{:S(2)}) collective-permute-start(bf16[304,384]{1,0:T(8,128)(2,1)S(1)} %add.133), channel_id=1, source_target_pairs={{0,8},{8,0},{16,24},{24,16},{1,9},{9,1},{17,25},{25,17},{2,10},{10... | collective-permute-start | bytes 700424 | tf_op jit(solution)/shard_map/ppermute | solution.py:670
  261.7 17.0 %all-to-all-start.1 = ((bf16[16,96,256]{2,1,0:T(8,128)(2,1)}), bf16[16,96,256]{2,1,0:T(8,128)(2,1)S(1)}, u32[]{:S(2)}, u32[]{:S(2)}) async-start(bf16[16,96,256]{2,1,0:T(8,128)(2,1)} %bitcast.38), calls=%async_computation.1 | async-start | bytes 1572864 | tf_op jit(solution)/shard_map/all_to_all | solution.py:673
  (90 other events, 668.8 us)
